TPU v7x, 32 devices: a whole 2x2x4 slice. The times are simulated.
32 devices in a mesh: loop: 4 (over y, x), wide: 8 (over z, core).
Axes of the slice: x: 2, y: 2, z: 4, core: 2. Of those that a mesh axis runs over, the one named last changes fastest.
Arguments:
- feats: bfloat16 [8, 1024, 256], P('wide', 'loop'), may hold values from -6 to 6
- w_first: bfloat16 [256, 1024], replicated, may hold values from -0.375 to 0.375
- w_second: bfloat16 [1024, 256], replicated, may hold values from -0.1875 to 0.1875
- cotangent: bfloat16 [8, 1024, 256], P('wide', 'loop'), may hold values from -0.15625 to 0.15625
- block_values: bfloat16 [4, 8, 80, 64, 64], P('loop', 'wide'), may hold values from -0.25 to 0.25
- row_ptr: int32 [4, 8, 17], P('loop', 'wide'), may hold values from 0 to 80, as said below
- col_idx: int32 [4, 8, 80], P('loop', 'wide'), may hold values from 0 to 31
Outputs:
- propagated: bfloat16 [8, 1024, 256], P('wide', 'loop')
- grad_first: float32 [256, 1024], P('wide')
- grad_second: float32 [1024, 256], P('wide')
Inputs may be any that keep to these rules, and one draw needn't show every extreme that they name: In each tile row_ptr starts at 0, never falls, and its last entry (the tile's live blocks) is at most 80; in every draw some tile has exactly 80 live blocks. `col_idx`: entries of empty slots are ignored.
All inputs are finite; a program needn't handle non-finite values.
Results may differ from a plain program's by a relative error of at most 0.02.
Values may be sent and summed in bfloat16 or wider, within the bound.
A program may use at most 128 MiB of HBM per device.

v0:
```python
import jax
import jax.numpy as jnp
from jax import lax
from jax.sharding import PartitionSpec as P

STEPS = 3


ALPHA = 0.1


def slot_layout(pointers, slot_total):
    slot_ids = jnp.arange(slot_total, dtype=jnp.int32)
    slot_row = jnp.sum((pointers[1:, None] <= slot_ids).astype(jnp.int32), axis=0)
    slot_live = (slot_ids < pointers[-1:]).astype(jnp.float32)
    return (jnp.minimum(slot_row, pointers.shape[0] - 2), slot_live)


def silu_slope(value):
    sigma = jax.nn.sigmoid(value)
    return sigma * (1.0 + value * (1.0 - sigma))


def block_sums(slot_target, products, row_count, block_size):
    targets = jnp.arange(row_count // block_size)
    one_hot = (slot_target[:, None] == targets[None, :]).astype(jnp.float32)
    landed = jnp.einsum("sr,sid->rid", one_hot, products, precision=lax.Precision.HIGHEST)
    return landed.reshape(row_count, products.shape[-1])


def propagate(current, teleport, tile_values, slot_row, slot_live, slot_col):
    block_size = tile_values.shape[-1]
    features = current.shape[-1]
    columns = lax.all_gather(current, "wide", axis=0, tiled=True)
    picked = columns.reshape(-1, block_size, features)[slot_col]
    products = (
        jnp.einsum("sij,sjd->sid", tile_values, picked, preferred_element_type=jnp.float32)
        * slot_live[:, None, None]
    )
    summed = lax.psum_scatter(
        block_sums(slot_row, products, current.shape[0] * lax.axis_size("loop"), block_size),
        "loop",
        scatter_dimension=0,
        tiled=True,
    )
    return ((1.0 - ALPHA) * summed + ALPHA * teleport.astype(jnp.float32)).astype(jnp.bfloat16)


def pull_back(adjoint_now, tile_values, slot_row, slot_live, slot_col):
    block_size = tile_values.shape[-1]
    features = adjoint_now.shape[-1]
    own_rows = adjoint_now.shape[0]
    whole_rows = lax.all_gather(adjoint_now, "loop", axis=0, tiled=True)
    picked = whole_rows.reshape(-1, block_size, features)[slot_row]
    products = (
        jnp.einsum("sij,sid->sjd", tile_values, picked, preferred_element_type=jnp.float32)
        * slot_live[:, None, None]
    )
    summed = lax.psum_scatter(
        block_sums(slot_col, products, own_rows * lax.axis_size("wide"), block_size),
        "wide",
        scatter_dimension=0,
        tiled=True,
    )
    return ((1.0 - ALPHA) * summed).astype(jnp.bfloat16)


def body(feats, w_first, w_second, cotangent, block_values, row_ptr, col_idx):
    tile_values = block_values[0, 0]
    slot_row, slot_live = slot_layout(row_ptr[0, 0], tile_values.shape[0])
    slot_col = col_idx[0, 0]
    flat_feats = feats[0]
    pre_act = jnp.dot(flat_feats, w_first, preferred_element_type=jnp.float32)
    hidden = jax.nn.silu(pre_act).astype(jnp.bfloat16)
    teleport = jnp.dot(hidden, w_second, preferred_element_type=jnp.float32).astype(jnp.bfloat16)
    current = teleport
    for _ in range(STEPS):
        current = propagate(current, teleport, tile_values, slot_row, slot_live, slot_col)
    adjoint_now = cotangent[0]
    collected = adjoint_now.astype(jnp.float32)
    for repeat in range(STEPS):
        adjoint_now = pull_back(adjoint_now, tile_values, slot_row, slot_live, slot_col)
        if repeat < STEPS - 1:
            collected = collected + adjoint_now.astype(jnp.float32)
    grad_teleport = (ALPHA * collected + adjoint_now.astype(jnp.float32)).astype(jnp.bfloat16)
    grad_hidden = lax.dot_general(
        grad_teleport, w_second, (((1,), (1,)), ((), ())), preferred_element_type=jnp.float32
    )
    grad_pre = (grad_hidden * silu_slope(pre_act)).astype(jnp.bfloat16)
    contract_items = (((0,), (0,)), ((), ()))
    piece = flat_feats
    first_part = lax.psum_scatter(
        lax.dot_general(piece, grad_pre, contract_items, preferred_element_type=jnp.float32).astype(
            jnp.bfloat16
        ),
        "wide",
        scatter_dimension=0,
        tiled=True,
    )
    piece = hidden
    second_part = lax.psum_scatter(
        lax.dot_general(
            piece, grad_teleport, contract_items, preferred_element_type=jnp.float32
        ).astype(jnp.bfloat16),
        "wide",
        scatter_dimension=0,
        tiled=True,
    )
    grad_first, grad_second = (
        lax.psum(first_part, "loop").astype(jnp.float32),
        lax.psum(second_part, "loop").astype(jnp.float32),
    )
    return (current[None], grad_first, grad_second)


def solution(mesh):
    return jax.shard_map(
        body,
        mesh=mesh,
        in_specs=(
            P("wide", "loop", None),
            P(),
            P(),
            P("wide", "loop", None),
            P("loop", "wide", None, None, None),
            P("loop", "wide", None),
            P("loop", "wide", None),
        ),
        out_specs=(P("wide", "loop", None), P("wide", None), P("wide", None)),
        check_vma=False,
    )
```

profile of v0, /device:TPU:0, one launch (start us, length us, event | category | flops | bytes accessed | tf_op | source)
XLA Modules:
  0.0 417.5 jit_solution(11266887082288069067)
XLA Ops:
  8.2 2.3 multiply_convert_fusion
  11.5 2.5 copy.33
  15.5 21.1 %all-gather.5.cloned.1.call-done = bf16[2048,256]{1,0:T(8,128)(2,1)} async-done(((bf16[256,256]{1,0:T(8,128)(2,1)}), bf16[2048,256]{1,0:T(8,128)(2,1)}) %all-gather.5.cloned.1.call-update) | async-done | bytes 1048592 | tf_op jit(solution)/shard_map/all_gather | solution.py:34
  36.6 3.6 gather_fusion
  40.2 2.7 multiply_bitcast_fusion.5
  43.0 4.8 %fusion.10 = f32[16,64,256]{2,0,1:T(8,128)S(1)} fusion(f32[80,64,256]{2,1,0:T(8,128)S(1)} %multiply_bitcast_fusion.5, s32[80]{0:T(128)S(1)} %broadcast_minimum_fusion), kind=kOutput, calls=%fused_computation.16 | convolution fusion | flops 251659520 | bytes 6291776 | tf_op jit(solution)/shard_map/sr,sid->rid/dot_general | solution.py:27
  47.8 1.6 copy.26
  49.4 12.9 %all-gather = bf16[1,1024,256]{2,1,0:T(8,128)(2,1)S(1)} all-gather(bf16[1,256,256]{2,1,0:T(8,128)(2,1)S(1)} %copy-done.8), channel_id=2, replica_groups=mesh['loop'=4,'wide'=8] {'loop'}, dimensions={1}, use_global_device_ids=true | all-gather | bytes 655360 | tf_op jit(solution)/shard_map/all_gather | solution.py:53
  62.4 2.4 gather_fusion.3
  64.8 2.6 multiply_bitcast_fusion.2
  67.4 5.0 %fusion.4 = f32[32,64,256]{2,0,1:T(8,128)S(1)} fusion(f32[80,64,256]{2,1,0:T(8,128)S(1)} %multiply_bitcast_fusion.2, s32[80]{0:T(128)S(1)} %bitcast.94), kind=kOutput, calls=%fused_computation.10 | convolution fusion | flops 503319040 | bytes 7340352 | tf_op jit(solution)/shard_map/sr,sid->rid/dot_general | solution.py:27
  72.4 2.5 copy.35
  75.0 2.4 reduce-scatter.11.cloned.1.call-done
  77.5 1.6 add_convert_fusion.2
  79.2 36.7 %reduce-scatter.17.cloned.1.call-done = f32[256,256]{1,0:T(8,128)} async-done(((f32[2048,256]{1,0:T(8,128)}), f32[256,256]{1,0:T(8,128)}) %reduce-scatter.17.cloned.1.call-update) | async-done | bytes 262160 | tf_op jit(solution)/shard_map/reduce_scatter | solution.py:59
  116.9 10.5 %all_gather.22 = bf16[1024,256]{1,0:T(8,128)(2,1)S(1)} all-gather(bf16[256,256]{1,0:T(8,128)(2,1)S(1)} %multiply_convert_fusion.3), channel_id=1, replica_groups=mesh['loop'=4,'wide'=8] {'loop'}, dimensions={0}, use_global_device_ids=true | all-gather | bytes 655360 | tf_op jit(solution)/shard_map/all_gather | solution.py:53
  127.4 2.4 gather_fusion.4
  129.8 2.6 multiply_bitcast_fusion.1
  132.3 5.0 %fusion.2 = f32[32,64,256]{2,0,1:T(8,128)S(1)} fusion(f32[80,64,256]{2,1,0:T(8,128)S(1)} %multiply_bitcast_fusion.1, s32[80]{0:T(128)S(1)} %bitcast.95), kind=kOutput, calls=%fused_computation.8 | convolution fusion | flops 503319040 | bytes 7340352 | tf_op jit(solution)/shard_map/sr,sid->rid/dot_general | solution.py:27
  137.4 2.6 copy.38
  140.5 3.6 gather_fusion.1
  144.1 2.7 multiply_bitcast_fusion.4
  146.9 4.8 %fusion.8 = f32[16,64,256]{2,0,1:T(8,128)S(1)} fusion(f32[80,64,256]{2,1,0:T(8,128)S(1)} %multiply_bitcast_fusion.4, s32[80]{0:T(128)S(1)} %broadcast_minimum_fusion), kind=kOutput, calls=%fused_computation.14 | convolution fusion | flops 251659520 | bytes 6291776 | tf_op jit(solution)/shard_map/sr,sid->rid/dot_general | solution.py:27
  151.7 1.6 copy.29
  153.3 23.3 %reduce-scatter.19.cloned.1.call-done = f32[256,256]{1,0:T(8,128)} async-done(((f32[2048,256]{1,0:T(8,128)}), f32[256,256]{1,0:T(8,128)}) %reduce-scatter.19.cloned.1.call-update) | async-done | bytes 262160 | tf_op jit(solution)/shard_map/reduce_scatter | solution.py:59
  177.6 12.8 %all_gather.23 = bf16[1024,256]{1,0:T(8,128)(2,1)S(1)} all-gather(bf16[256,256]{1,0:T(8,128)(2,1)S(1)} %multiply_convert_fusion.2), channel_id=1, replica_groups=mesh['loop'=4,'wide'=8] {'loop'}, dimensions={0}, use_global_device_ids=true | all-gather | bytes 655360 | tf_op jit(solution)/shard_map/all_gather | solution.py:53
  190.4 2.4 gather_fusion.5
  192.8 2.6 multiply_bitcast_fusion
  195.4 5.0 %fusion = f32[32,64,256]{2,0,1:T(8,128)S(1)} fusion(f32[80,64,256]{2,1,0:T(8,128)S(1)} %multiply_bitcast_fusion, s32[80]{0:T(128)S(1)} %bitcast.96), kind=kOutput, calls=%fused_computation.6 | convolution fusion | flops 503319040 | bytes 7340352 | tf_op jit(solution)/shard_map/sr,sid->rid/dot_general | solution.py:27
  200.4 2.5 copy.41
  203.1 2.6 reduce-scatter.13.cloned.1.call-done
  205.7 1.6 add_convert_fusion.1
  207.4 36.7 %reduce-scatter.21.cloned.1.call-done = f32[256,256]{1,0:T(8,128)} async-done(((f32[2048,256]{1,0:T(8,128)}), f32[256,256]{1,0:T(8,128)}) %reduce-scatter.21.cloned.1.call-update) | async-done | bytes 262160 | tf_op jit(solution)/shard_map/reduce_scatter | solution.py:59
  245.1 2.0 fusion.13
  248.2 1.1 convolution_convert_fusion
  249.6 17.3 %all-gather.9.cloned.1.call-done = bf16[2048,256]{1,0:T(8,128)(2,1)} async-done(((bf16[256,256]{1,0:T(8,128)(2,1)}), bf16[2048,256]{1,0:T(8,128)(2,1)}) %all-gather.9.cloned.1.call-update) | async-done | bytes 1048592 | tf_op jit(solution)/shard_map/all_gather | solution.py:34
  266.9 3.6 gather_fusion.2
  270.5 2.8 multiply_bitcast_fusion.3
  273.3 4.8 %fusion.6 = f32[16,64,256]{2,0,1:T(8,128)S(1)} fusion(f32[80,64,256]{2,1,0:T(8,128)S(1)} %multiply_bitcast_fusion.3, s32[80]{0:T(128)S(1)} %broadcast_minimum_fusion), kind=kOutput, calls=%fused_computation.12 | convolution fusion | flops 251659520 | bytes 6291776 | tf_op jit(solution)/shard_map/sr,sid->rid/dot_general | solution.py:27
  278.1 1.6 copy.32
  279.8 20.3 %reduce-scatter.25.cloned.1.call-done = bf16[32,1024]{1,0:T(8,128)(2,1)} async-done(((bf16[256,1024]{1,0:T(8,128)(2,1)}), bf16[32,1024]{1,0:T(8,128)(2,1)}) %reduce-scatter.25.cloned.1.call-update) | async-done | bytes 65552
  300.0 1.7 copy.44
  301.7 29.9 %reduce-scatter.23.cloned.1.call-done = bf16[128,256]{1,0:T(8,128)(2,1)} async-done(((bf16[1024,256]{1,0:T(8,128)(2,1)}), bf16[128,256]{1,0:T(8,128)(2,1)}) %reduce-scatter.23.cloned.1.call-update) | async-done | bytes 65552 | tf_op jit(solution)/shard_map/reduce_scatter | solution.py:101
  331.6 29.1 %reduce-scatter.15.cloned.1.call-done = f32[256,256]{1,0:T(8,128)} async-done(((f32[1024,256]{1,0:T(8,128)}), f32[256,256]{1,0:T(8,128)}) %reduce-scatter.15.cloned.1.call-update) | async-done | bytes 262160 | tf_op jit(solution)/shard_map/reduce_scatter | solution.py:40
  360.7 1.6 fusion.23
  362.3 44.8 %all-reduce.3.cloned.1.call-done = (bf16[32,1024]{0,1:T(8,128)(2,1)}, bf16[128,256]{1,0:T(8,128)(2,1)}) async-done(((bf16[32,1024]{0,1:T(8,128)(2,1)}, bf16[128,256]{1,0:T(8,128)(2,1)}), (bf16[32,1024]{0,1:T(8,128)(2,1)}, bf16[128,256]{1,0:T(8,128)(2,1)})) %all-reduce.3.cloned.1.call-update) | async-done | bytes 131088 | tf_op jit(solution)/shard_map/psum | solution.py:110
  407.2 1.5 convert_element_type.99
  408.7 1.7 copy.42
  (63 shorter events, 8.8 us)
Async XLA Ops:
  7.2 1.1 copy-start
  7.2 3.3 copy-start.6
  7.2 4.3 %copy-start.3 = (bf16[1,1,80,64,64]{2,4,3,1,0:T(8,128)(2,1)S(1)}, bf16[1,1,80,64,64]{2,4,3,1,0:T(8,128)(2,1)}, u32[]{:S(2)}) copy-start(bf16[1,1,80,64,64]{2,4,3,1,0:T(8,128)(2,1)} %param.11) | copy-start | bytes 1966084
  7.2 29.4 %all-gather.5.cloned.1.call-start = ((), (), s32[]{:S(2)}) async-start(), calls=%async_computation.8 | async-start | bytes 1179648 | tf_op jit(solution)/shard_map/all_gather | solution.py:34
  10.5 3.6 copy-start.11
  10.5 4.8 %copy-start.9 = (s32[1,1,80]{2,1,0:T(1,128)S(1)}, s32[1,1,80]{2,1,0:T(1,128)}, u32[]{:S(2)}) copy-start(s32[1,1,80]{2,1,0:T(1,128)} %param.13) | copy-start | bytes 964
  11.5 66.0 %reduce-scatter.11.cloned.1.call-start = ((), (), s32[]{:S(2)}) async-start(), calls=%async_computation.9 | async-start | bytes 1310720 | tf_op jit(solution)/shard_map/reduce_scatter | solution.py:40
  47.8 1.7 copy-start.8
  49.4 66.5 %reduce-scatter.17.cloned.1.call-start = ((), (), s32[]{:S(2)}) async-start(), calls=%async_computation.14 | async-start | bytes 2359296 | tf_op jit(solution)/shard_map/reduce_scatter | solution.py:59
  72.4 5.1 %copy-start.2 = (bf16[256,256]{1,0:T(8,128)(2,1)S(1)}, bf16[256,256]{1,0:T(8,128)(2,1)}, u32[]{:S(2)}) copy-start(bf16[256,256]{1,0:T(8,128)(2,1)} %convolution_convert_fusion.2) | copy-start | bytes 393220
  75.0 65.5 %all-gather.7.cloned.1.call-start = ((), (), s32[]{:S(2)}) async-start(), calls=%async_computation.10 | async-start | bytes 1179648 | tf_op jit(solution)/shard_map/all_gather | solution.py:34
  79.1 97.5 %reduce-scatter.19.cloned.1.call-start = ((), (), s32[]{:S(2)}) async-start(), calls=%async_computation.15 | async-start | bytes 2359296 | tf_op jit(solution)/shard_map/reduce_scatter | solution.py:59
  140.0 65.7 %reduce-scatter.13.cloned.1.call-start = ((), (), s32[]{:S(2)}) async-start(), calls=%async_computation.11 | async-start | bytes 1310720 | tf_op jit(solution)/shard_map/reduce_scatter | solution.py:40
  153.3 90.8 %reduce-scatter.21.cloned.1.call-start = ((), (), s32[]{:S(2)}) async-start(), calls=%async_computation.16 | async-start | bytes 2359296 | tf_op jit(solution)/shard_map/reduce_scatter | solution.py:59
  200.4 43.7 %copy-start.4 = (f32[256,256]{1,0:T(8,128)S(1)}, f32[256,256]{1,0:T(8,128)}, u32[]{:S(2)}) copy-start(f32[256,256]{1,0:T(8,128)} %reduce-scatter.17.cloned.1.call-done) | copy-start | bytes 786436
  200.4 43.7 %copy-start.5 = (f32[256,256]{1,0:T(8,128)S(1)}, f32[256,256]{1,0:T(8,128)}, u32[]{:S(2)}) copy-start(f32[256,256]{1,0:T(8,128)} %reduce-scatter.19.cloned.1.call-done) | copy-start | bytes 786436
  203.0 42.1 %copy-start.7 = (bf16[1024,256]{1,0:T(8,128)(2,1)S(1)}, bf16[1024,256]{1,0:T(8,128)(2,1)}, u32[]{:S(2)}) copy-start(bf16[1024,256]{1,0:T(8,128)(2,1)} %param.9) | copy-start | bytes 1572868
  203.0 42.1 %copy-start.10 = (bf16[1,256,256]{2,1,0:T(8,128)(2,1)S(1)}, bf16[1,256,256]{2,1,0:T(8,128)(2,1)}, u32[]{:S(2)}) copy-start(bf16[1,256,256]{2,1,0:T(8,128)(2,1)} %param.7) | copy-start | bytes 393220
  203.0 63.9 %all-gather.9.cloned.1.call-start = ((), (), s32[]{:S(2)}) async-start(), calls=%async_computation.12 | async-start | bytes 1179648 | tf_op jit(solution)/shard_map/all_gather | solution.py:34
  207.3 92.7 %reduce-scatter.25.cloned.1.call-start = ((), (), s32[]{:S(2)}) async-start(), calls=%async_computation.18 | async-start | bytes 589824
  248.1 83.5 %reduce-scatter.23.cloned.1.call-start = ((), (), s32[]{:S(2)}) async-start(), calls=%async_computation.17 | async-start | bytes 589824 | tf_op jit(solution)/shard_map/reduce_scatter | solution.py:101
  249.4 111.3 %reduce-scatter.15.cloned.1.call-start = ((), (), s32[]{:S(2)}) async-start(), calls=%async_computation.13 | async-start | bytes 1310720 | tf_op jit(solution)/shard_map/reduce_scatter | solution.py:40
  273.3 137.2 %copy-start.1 = (bf16[256,1024]{1,0:T(8,128)(2,1)S(1)}, bf16[256,1024]{1,0:T(8,128)(2,1)}, u32[]{:S(2)}) copy-start(bf16[256,1024]{1,0:T(8,128)(2,1)} %param.8) | copy-start | bytes 1572868
  279.7 127.5 %all-reduce.3.cloned.1.call-start = ((), (), s32[]{:S(2)}) async-start(), calls=%async_computation.19 | async-start | bytes 655360 | tf_op jit(solution)/shard_map/psum | solution.py:110
Sparse Core Ops, SparseCore 0:
  11.6 24.9 all-gather.4
  49.5 27.9 reduce-scatter.10
  79.8 36.0 reduce-scatter.16
  117.9 20.7 all-gather.6
  140.9 35.7 reduce-scatter.18
  179.4 26.2 reduce-scatter.12
  208.0 36.0 reduce-scatter.20
  246.2 20.6 all-gather.8
  269.2 30.8 reduce-scatter.24
  302.1 29.4 reduce-scatter.22
  334.5 26.1 reduce-scatter.14
  363.5 43.6 all-reduce.2
where the time goes:
time: 426 us; the launch traced here: 417 us
  waiting for transfers between devices  264 us (62%)
  matrix products  51.8 us (12%)
  local copies, waits for them, and re-layouts  39.1 us (9%)
  blocking collectives  36.3 us (9%)
  between operations  14.7 us (3%)
  other arithmetic  10.2 us (2%)
    reduce_scatter x3, waiting for transfers between devices, pull_back(): lax.psum_scatter(block_sums(slot_col, products, own_rows * lax.axis_size(...  96.7 us
    psum x1, waiting for transfers between devices, body(): lax.psum(first_part, 'loop').astype(jnp.float32)  44.8 us
    all_gather x3, waiting for transfers between devices, propagate(): columns = lax.all_gather(current, 'wide', axis=0, tiled=True)  38.3 us
    all_gather x3, blocking collectives, pull_back(): whole_rows = lax.all_gather(adjoint_now, 'loop', axis=0, tiled=True)  36.3 us
    reduce_scatter x3, waiting for transfers between devices, propagate(): lax.psum_scatter(block_sums(slot_row, products, current.shape[0] * lax.ax...  34.1 us
    reduce_scatter x1, waiting for transfers between devices, body(): lax.psum_scatter(lax.dot_general(piece, grad_teleport, contract_items, pr...  29.9 us
    dot_general x6, matrix products, block_sums(): jnp.einsum('sr,sid->rid', one_hot, products, precision=lax.Precision.HIGH...  29.5 us
    unnamed x13, waiting for transfers between devices  20.5 us
  transfers between devices with their start and end apart: 12, of which 11 were waited for; matrix products, arithmetic and copies ran while one was open for 19% of the time, Pallas kernels for 0%

commit v1 on v0

v1 whole, which is shorter than its diff:
```python
import functools

import jax
import jax.numpy as jnp
from jax import lax
from jax.experimental import pallas as pl
from jax.experimental.pallas import tpu as pltpu
from jax.sharding import PartitionSpec as P

STEPS = 3


ALPHA = 0.1

MESH = pl.DeviceIdType.MESH


def silu_slope(value):
    sigma = jax.nn.sigmoid(value)
    return sigma * (1.0 + value * (1.0 - sigma))


def dense_kernel(index_ref, core_ref, mine_ref, other_ref, out_ref, acc):
    which, strip = pl.program_id(0), pl.program_id(1)
    chips, rows, cols = out_ref.shape[1], out_ref.shape[3], out_ref.shape[4]
    blk = mine_ref.shape[-1]
    per_strip = rows // blk
    per_chip = cols // (2 * blk)
    upper = lax.broadcasted_iota(jnp.int32, (blk, 2 * blk), 1) // blk
    pointers = index_ref.shape[1] - mine_ref.shape[0]

    def fill(values_ref, tile):
        for row in range(per_strip):
            acc[...] = jnp.zeros_like(acc)
            first = index_ref[tile, strip * per_strip + row]
            last = index_ref[tile, strip * per_strip + row + 1]

            def add(slot, carry):
                col = index_ref[tile, pointers + slot]
                block = values_ref[slot].astype(jnp.float32)
                wide = jnp.concatenate([block, block], axis=1)
                wide = jnp.where(upper == col % 2, wide, 0.0)
                acc[col // 2] = acc[col // 2] + wide
                return carry

            lax.fori_loop(first, last, add, 0)
            for chip in range(chips):
                for part in range(per_chip):
                    out_ref[
                        0, chip, 0, row * blk : (row + 1) * blk, part * 2 * blk : (part + 1) * 2 * blk
                    ] = acc[chip * per_chip + part].astype(out_ref.dtype)

    @pl.when(which == 0)
    def _():
        fill(mine_ref, 0)

    @pl.when(which == 1)
    def _():
        fill(other_ref, 1)


def dense_pair(index, core, mine, other, n_loop, n_chip, items):
    blk = mine.shape[-1]
    cols = 2 * items
    return pl.pallas_call(
        dense_kernel,
        out_shape=jax.ShapeDtypeStruct((n_loop, n_chip, 2, items, cols), jnp.bfloat16),
        grid_spec=pltpu.PrefetchScalarGridSpec(
            num_scalar_prefetch=2,
            grid=(2, n_loop),
            in_specs=[pl.BlockSpec(mine.shape, lambda u, s, idx, core: (0, 0, 0))] * 2,
            out_specs=pl.BlockSpec(
                (1, n_chip, 1, items, cols),
                lambda u, s, idx, core: (s, 0, u + core[0] - 2 * u * core[0], 0, 0),
            ),
            scratch_shapes=[pltpu.VMEM((n_chip * cols // (2 * blk), blk, 2 * blk), jnp.float32)],
        ),
        name="dense_pair",
    )(index, core, mine, other)


def power_kernel(
    n_loop, n_chip, tele_ref, cot_ref, dense_ref, prop_ref, gt_ref,
    tiles, zc, gr, ps, pr, qs, qr, prop_x, gt_x, prop_s, gt_s,
    tile_sem, ex_send, ex_recv, z_send, z_recv, g_send, g_recv, p_send, p_recv, q_send, q_recv,
):
    l = lax.axis_index("loop")
    w = lax.axis_index("wide")
    z, c = w // 2, w % 2
    oc = 1 - c
    items, half = tele_ref.shape[1], tele_ref.shape[2]
    load = pltpu.make_async_copy(dense_ref, tiles, tile_sem)
    load.start()

    barrier = pltpu.get_barrier_semaphore()
    partner = (l, 2 * z + oc)
    chip_peers = [lax.rem(z + j, n_chip) for j in range(1, n_chip)]
    loop_peers = [lax.rem(l + j, n_loop) for j in range(1, n_loop)]
    pl.semaphore_signal(barrier, inc=1, device_id=partner, device_id_type=MESH)
    for zp in chip_peers:
        pl.semaphore_signal(barrier, inc=1, device_id=(l, 2 * zp + c), device_id_type=MESH)
    for lp in loop_peers:
        pl.semaphore_signal(barrier, inc=1, device_id=(lp, w), device_id_type=MESH)
    pl.semaphore_wait(barrier, n_loop + n_chip - 1)

    def remote(src, dst, send, recv, target):
        return pltpu.make_async_remote_copy(
            src_ref=src, dst_ref=dst, send_sem=send, recv_sem=recv,
            device_id=target, device_id_type=MESH,
        )

    def z_copy(k, slot, target):
        return remote(zc.at[k, slot], zc.at[k, slot], z_send.at[k, target], z_recv.at[k, slot], (l, 2 * target + c))

    def g_copy(k, slot, target):
        return remote(gr.at[k, slot], gr.at[k, slot], g_send.at[k, target], g_recv.at[k, slot], (target, w))

    def p_copy(k, slot, target):
        return remote(ps.at[k, target], pr.at[k, slot], p_send.at[k, target], p_recv.at[k, slot], (target, w))

    def q_copy(k, slot, target):
        return remote(qs.at[k, target], qr.at[k, slot], q_send.at[k, target], q_recv.at[k, slot], (l, 2 * target + c))

    cot_x = remote(cot_ref.at[oc], gr.at[0, l, c], ex_send.at[1], ex_recv.at[1], partner)
    cot_x.start()
    tele_x = remote(tele_ref.at[oc], zc.at[0, z, c], ex_send.at[0], ex_recv.at[0], partner)
    tele_x.start()
    gr[0, l, c] = cot_ref[c]
    zc[0, z, c] = tele_ref[c]
    cot_x.wait()
    for lp in loop_peers:
        g_copy(0, l, lp).start()
    tele_x.wait()
    for zp in chip_peers:
        z_copy(0, z, zp).start()
    load.wait()

    def forward_part(k, lp):
        total = None
        for zp in range(n_chip):
            part = jnp.dot(
                tiles[lp, zp].reshape(2 * items, 2 * items),
                zc[k, zp].reshape(2 * items, half),
                preferred_element_type=jnp.float32,
            )
            total = part if total is None else total + part
        return total

    def adjoint_part(k, zp):
        total = None
        for lp in range(n_loop):
            for t in range(2):
                part = jnp.dot(gr[k, lp, t], tiles[lp, zp, t], preferred_element_type=jnp.float32)
                total = part if total is None else total + part
        return total

    for k in range(STEPS):
        for lp in loop_peers:
            g_copy(k, lp, l).wait_recv()

        def q_step(j, carry):
            zp = lax.rem(z + 1 + j, n_chip)
            value = adjoint_part(k, zp).astype(jnp.bfloat16)
            for t in range(2):
                qs[k, zp, t] = value[:, t * items : (t + 1) * items]
            q_copy(k, z, zp).start()
            return carry

        lax.fori_loop(0, n_chip - 1, q_step, 0)
        own_q = adjoint_part(k, z)

        for zp in chip_peers:
            z_copy(k, zp, z).wait_recv()

        def p_step(j, carry):
            lp = lax.rem(l + 1 + j, n_loop)
            ps[k, lp] = forward_part(k, lp).astype(jnp.bfloat16)
            p_copy(k, l, lp).start()
            return carry

        lax.fori_loop(0, n_loop - 1, p_step, 0)
        own_p = forward_part(k, l)

        for zp in chip_peers:
            q_copy(k, zp, z).wait_recv()
        for t in range(2):
            total = own_q[:, t * items : (t + 1) * items]
            for zp in chip_peers:
                total = total + qr[k, zp, t].astype(jnp.float32)
            gr[k + 1, l, t] = ((1.0 - ALPHA) * total).astype(jnp.bfloat16)
        if k < STEPS - 1:
            for lp in loop_peers:
                g_copy(k + 1, l, lp).start()
        else:
            for t in range(2):
                kept = gr[0, l, t].astype(jnp.float32)
                for step in range(1, STEPS):
                    kept = kept + gr[step, l, t].astype(jnp.float32)
                gt_s[t] = (ALPHA * kept + gr[STEPS, l, t].astype(jnp.float32)).astype(jnp.bfloat16)
            gt_copy = remote(gt_s.at[oc], gt_x, ex_send.at[3], ex_recv.at[3], partner)
            gt_copy.start()

        for lp in loop_peers:
            p_copy(k, lp, l).wait_recv()
        total = own_p
        for lp in loop_peers:
            total = total + pr[k, lp].astype(jnp.float32)
        teleport = zc[0, z].reshape(2 * items, half).astype(jnp.float32)
        mixed = ((1.0 - ALPHA) * total + ALPHA * teleport).astype(jnp.bfloat16)
        if k < STEPS - 1:
            for t in range(2):
                zc[k + 1, z, t] = mixed[t * items : (t + 1) * items]
            for zp in chip_peers:
                z_copy(k + 1, z, zp).start()
        else:
            for t in range(2):
                prop_s[t] = mixed[t * items : (t + 1) * items]
            prop_copy = remote(prop_s.at[oc], prop_x, ex_send.at[2], ex_recv.at[2], partner)
            prop_copy.start()

    for k in range(STEPS):
        for zp in chip_peers:
            z_copy(k, z, zp).wait_send()
            q_copy(k, z, zp).wait_send()
        for lp in loop_peers:
            g_copy(k, l, lp).wait_send()
            p_copy(k, l, lp).wait_send()
    gt_copy.wait()
    gt_ref[c] = gt_s[c]
    gt_ref[oc] = gt_x[...]
    prop_copy.wait()
    prop_ref[c] = prop_s[c]
    prop_ref[oc] = prop_x[...]


def power_steps(tele, cot, dense, n_loop, n_chip):
    _, items, half = tele.shape
    bf16, dma = jnp.bfloat16, pltpu.SemaphoreType.DMA
    vmem = pl.BlockSpec(memory_space=pltpu.VMEM)
    return pl.pallas_call(
        functools.partial(power_kernel, n_loop, n_chip),
        out_shape=(
            jax.ShapeDtypeStruct((2, items, half), bf16),
            jax.ShapeDtypeStruct((2, half, items), bf16),
        ),
        in_specs=[vmem, vmem, pl.BlockSpec(memory_space=pl.ANY)],
        out_specs=(vmem, vmem),
        scratch_shapes=[
            pltpu.VMEM(dense.shape, bf16),
            pltpu.VMEM((STEPS, n_chip, 2, items, half), bf16),
            pltpu.VMEM((STEPS + 1, n_loop, 2, half, items), bf16),
            pltpu.VMEM((STEPS, n_loop, 2 * items, half), bf16),
            pltpu.VMEM((STEPS, n_loop, 2 * items, half), bf16),
            pltpu.VMEM((STEPS, n_chip, 2, half, items), bf16),
            pltpu.VMEM((STEPS, n_chip, 2, half, items), bf16),
            pltpu.VMEM((items, half), bf16),
            pltpu.VMEM((half, items), bf16),
            pltpu.VMEM((2, items, half), bf16),
            pltpu.VMEM((2, half, items), bf16),
            dma,
            dma((4,)),
            dma((4,)),
            dma((STEPS, n_chip)),
            dma((STEPS, n_chip)),
            dma((STEPS, n_loop)),
            dma((STEPS, n_loop)),
            dma((STEPS, n_loop)),
            dma((STEPS, n_loop)),
            dma((STEPS, n_chip)),
            dma((STEPS, n_chip)),
        ],
        compiler_params=pltpu.CompilerParams(
            collective_id=0, has_side_effects=True, vmem_limit_bytes=60 * 2**20
        ),
        name="power_steps",
    )(tele, cot, dense)


def body(feats, w_first, w_second, cotangent, block_values, row_ptr, col_idx):
    n_loop, n_wide = lax.axis_size("loop"), lax.axis_size("wide")
    n_chip = n_wide // 2
    mine = block_values[0, 0]
    index = jnp.concatenate([row_ptr[0, 0], col_idx[0, 0]])
    swap = [(i, i + 1 - 2 * (i % 2)) for i in range(n_wide)]
    other = lax.ppermute(mine, "wide", swap)
    other_index = lax.ppermute(index, "wide", swap)
    flat_feats = feats[0]
    items, features = flat_feats.shape
    half = features // 2
    pre_act = jnp.dot(flat_feats, w_first, preferred_element_type=jnp.float32)
    hidden = jax.nn.silu(pre_act).astype(jnp.bfloat16)
    teleport = jnp.dot(hidden, w_second, preferred_element_type=jnp.float32).astype(jnp.bfloat16)
    core = lax.rem(lax.axis_index("wide"), 2).astype(jnp.int32).reshape(1)
    dense = dense_pair(
        jnp.stack([index, other_index]), core, mine, other, n_loop, n_chip, items
    )
    prop_halves, gt_flipped = power_steps(
        teleport.reshape(items, 2, half).transpose(1, 0, 2),
        cotangent[0].T.reshape(2, half, items),
        dense,
        n_loop,
        n_chip,
    )
    current = prop_halves.transpose(1, 0, 2).reshape(items, features)
    grad_teleport = gt_flipped.reshape(features, items).T
    grad_hidden = lax.dot_general(
        grad_teleport, w_second, (((1,), (1,)), ((), ())), preferred_element_type=jnp.float32
    )
    grad_pre = (grad_hidden * silu_slope(pre_act)).astype(jnp.bfloat16)
    contract_items = (((0,), (0,)), ((), ()))
    first_part = lax.psum_scatter(
        lax.dot_general(
            flat_feats, grad_pre, contract_items, preferred_element_type=jnp.float32
        ).astype(jnp.bfloat16),
        "wide",
        scatter_dimension=0,
        tiled=True,
    )
    second_part = lax.psum_scatter(
        lax.dot_general(
            hidden, grad_teleport, contract_items, preferred_element_type=jnp.float32
        ).astype(jnp.bfloat16),
        "wide",
        scatter_dimension=0,
        tiled=True,
    )
    grad_first, grad_second = (
        lax.psum(first_part, "loop").astype(jnp.float32),
        lax.psum(second_part, "loop").astype(jnp.float32),
    )
    return (current[None], grad_first, grad_second)


def solution(mesh):
    return jax.shard_map(
        body,
        mesh=mesh,
        in_specs=(
            P("wide", "loop", None),
            P(),
            P(),
            P("wide", "loop", None),
            P("loop", "wide", None, None, None),
            P("loop", "wide", None),
            P("loop", "wide", None),
        ),
        out_specs=(P("wide", "loop", None), P("wide", None), P("wide", None)),
        check_vma=False,
    )
```

time: 426 us -> 239 us (0.56); the launches traced: 417 us -> 237 us
  waiting for transfers between devices: 264 us -> 111 us
  Pallas kernels: 0 us -> 89.7 us
  matrix products: 51.8 us -> 4.89 us
  blocking collectives: 36.3 us -> 0 us
  local copies, waits for them, and re-layouts: 39.1 us -> 13.2 us
  other arithmetic: 10.2 us -> 3.62 us
    reduce_scatter x7 -> x1, waiting for transfers between devices: 161 us -> 30.3 us  [body(): lax.psum_scatter(lax.dot_general(hidden, grad_teleport, contract_items, p...]
    pallas_call x0 -> x2, Pallas kernels: none -> 89.7 us  [the longest x1 79.6 us: power_steps(): pl.pallas_call(functools.partial(power_kernel, n_loop, n_chip), out_shape...]
    dot_general x14 -> x2, matrix products: 48.6 us -> 3.19 us  [the longest x1 2.04 us: body(): lax.dot_general(flat_feats, grad_pre, contract_items, preferred_element_t...]
    all_gather x3 -> x0, waiting for transfers between devices: 38.3 us -> none  [propagate(): columns = lax.all_gather(current, 'wide', axis=0, tiled=True)]
    all_gather x3 -> x0, blocking collectives: 36.3 us -> none  [pull_back(): whole_rows = lax.all_gather(adjoint_now, 'loop', axis=0, tiled=True)]
    gather x6 -> x0, local copies, waits for them, and re-layouts: 18 us -> none  [the longest x3 10.8 us: propagate(): picked = columns.reshape(-1, block_size, features)[slot_col]]
    unnamed x13 -> x4, waiting for transfers between devices: 20.5 us -> 37.3 us
    dot_general x6 -> x0, local copies, waits for them, and re-layouts: 12.4 us -> none  [block_sums(): jnp.einsum('sr,sid->rid', one_hot, products, precision=lax.Precision.HIGH...]
  transfers between devices with their start and end apart: 12 -> 5, of which waited for: 11 -> 3; matrix products, arithmetic and copies ran while one was open for 19% -> 5% of each run, Pallas kernels for 0% -> 0%
where the time goes in v1:
time: 239 us; the launch traced here: 237 us
  waiting for transfers between devices  111 us (46%)
  Pallas kernels  89.7 us (38%)
  between operations  13.8 us (6%)
  local copies, waits for them, and re-layouts  13.2 us (6%)
  matrix products  4.89 us (2%)
  other arithmetic  3.62 us (2%)
    pallas_call x1, Pallas kernels, power_steps(): pl.pallas_call(functools.partial(power_kernel, n_loop, n_chip), out_shape...  79.6 us
    psum x1, waiting for transfers between devices, body(): lax.psum(first_part, 'loop').astype(jnp.float32)  43.8 us
    unnamed x4, waiting for transfers between devices  37.3 us
    reduce_scatter x1, waiting for transfers between devices, body(): lax.psum_scatter(lax.dot_general(hidden, grad_teleport, contract_items, p...  30.3 us
    pallas_call x1, Pallas kernels, dense_pair(): pl.pallas_call(dense_kernel, out_shape=jax.ShapeDtypeStruct((n_loop, n_ch...  10.1 us
    unnamed x17, local copies, waits for them, and re-layouts  8.88 us
  transfers between devices with their start and end apart: 5, of which 3 were waited for; matrix products, arithmetic and copies ran while one was open for 5% of the time, Pallas kernels for 0%

profile of v1, /device:TPU:0, one launch (start us, length us, event | category | flops | bytes accessed | tf_op | source)
XLA Modules:
  0.0 237.4 jit_solution(7858333211789208830)
XLA Ops:
  7.2 0.0 copy-start
  7.2 0.0 copy-start.5
  7.2 0.0 reduce-scatter.7.cloned.1.call-start
  7.2 0.8 pad_add_fusion.1
  8.0 0.5 collective-permute-start
  8.5 0.1 collective-permute-start.1
  8.6 0.7 fusion.18
  9.3 3.7 %copy.21 = bf16[1,1,80,64,64]{4,3,2,1,0:T(8,128)(2,1)} copy(bf16[1,1,80,64,64]{2,4,3,1,0:T(8,128)(2,1)} %param.11) | data formatting | bytes 1310720 | tf_op args[4]
  13.0 0.0 copy-done
  13.0 0.0 copy-done.5
  13.0 0.0 copy-start.1
  13.0 1.3 multiply_convert_fusion
  14.4 0.0 copy-start.3
  14.4 0.0 copy-done.1
  14.4 0.3 convolution_convert_fusion.2
  14.7 0.8 copy.19
  15.5 0.0 copy-done.3
  15.5 0.8 copy.20
  16.3 0.0 collective-permute-done
  16.3 0.6 pad_add_fusion.index_ref
  16.8 0.0 collective-permute-done.1
  16.8 2.7 %copy.23.other_ref = bf16[80,64,64]{2,1,0:T(8,128)(2,1)} copy(bf16[80,64,64]{0,2,1:T(8,128)(2,1)S(1)} %collective-permute-done.1) | data formatting | bytes 1310720 | tf_op jit(solution)/shard_map/ppermute | solution.py:285
  19.6 10.1 %dense_pair.1.dense_ref = bf16[4,4,2,256,512]{4,3,2,1,0:T(8,128)(2,1)} custom-call(s32[2,97]{1,0:T(2,128)} %pad_add_fusion.index_ref, s32[1]{0:T(128)} %bitcast.10.core_ref, bf16[80,64,64]{2,1,0:T(8,128)(2,1)} %bitcast.34, bf16[80,64,64]{2,1,0:T(8,128)(2,1)} %copy.23.other_ref), custom_call_target="tpu_custom_call" | custom-call | tf_op jit(solution)/shard_map/dense_pair/pallas_call | solution.py:65
  29.6 79.6 %power_steps.1 = (bf16[2,256,128]{2,1,0:T(8,128)(2,1)}, bf16[2,128,256]{2,1,0:T(8,128)(2,1)}) custom-call(bf16[2,256,128]{2,1,0:T(8,128)(2,1)} %bitcast.36, bf16[2,128,256]{2,1,0:T(8,128)(2,1)} %bitcast.37, bf16[4,4,2,256,512]{4,3,2,1,0:T(8,128)(2,1)} %dense_pair.1.dense_ref), custom_call_target="tpu_custom_call" | custom-call | tf_op jit(solution)/shard_map/power_steps/pallas_call | solution.py:240
  109.2 2.0 fusion.1
  111.3 0.0 copy-start.2
  111.3 1.0 copy.28
  112.3 0.0 reduce-scatter.7.cloned.1.call-update
  112.3 0.0 copy-start.4
  112.3 0.0 reduce-scatter.5.cloned.1.call-start
  112.4 0.0 copy-done.2
  112.4 1.2 convolution_convert_fusion
  113.6 0.0 reduce-scatter.5.cloned.1.call-update
  113.6 0.0 all-reduce.3.cloned.1.call-start
  113.6 37.3 %reduce-scatter.7.cloned.1.call-done = bf16[32,1024]{1,0:T(8,128)(2,1)} async-done(((bf16[256,1024]{1,0:T(8,128)(2,1)}), bf16[32,1024]{1,0:T(8,128)(2,1)}) %reduce-scatter.7.cloned.1.call-update) | async-done | bytes 65552
  150.9 1.7 copy.29
  152.6 30.3 %reduce-scatter.5.cloned.1.call-done = bf16[128,256]{1,0:T(8,128)(2,1)} async-done(((bf16[1024,256]{1,0:T(8,128)(2,1)}), bf16[128,256]{1,0:T(8,128)(2,1)}) %reduce-scatter.5.cloned.1.call-update) | async-done | bytes 65552 | tf_op jit(solution)/shard_map/reduce_scatter | solution.py:319
  182.9 0.0 all-reduce.3.cloned.1.call-update
  183.0 0.0 copy-done.4
  183.0 0.1 copy.24
  183.1 0.8 copy.25
  183.8 43.8 %all-reduce.3.cloned.1.call-done = (bf16[32,1024]{0,1:T(8,128)(2,1)}, bf16[128,256]{1,0:T(8,128)(2,1)}) async-done(((bf16[32,1024]{0,1:T(8,128)(2,1)}, bf16[128,256]{1,0:T(8,128)(2,1)}), (bf16[32,1024]{0,1:T(8,128)(2,1)}, bf16[128,256]{1,0:T(8,128)(2,1)})) %all-reduce.3.cloned.1.call-update) | async-done | bytes 131088 | tf_op jit(solution)/shard_map/psum | solution.py:328
  227.7 1.5 convert_element_type.31
  229.2 1.7 copy.26
Async XLA Ops:
  7.2 5.9 %copy-start = (bf16[256,1024]{1,0:T(8,128)(2,1)S(1)}, bf16[256,1024]{1,0:T(8,128)(2,1)}, u32[]{:S(2)}) copy-start(bf16[256,1024]{1,0:T(8,128)(2,1)} %param.8) | copy-start | bytes 1572868
  7.2 5.8 %copy-start.5 = (bf16[1,256,256]{2,1,0:T(8,128)(2,1)S(1)}, bf16[1,256,256]{2,1,0:T(8,128)(2,1)}, u32[]{:S(2)}) copy-start(bf16[1,256,256]{2,1,0:T(8,128)(2,1)} %param.7) | copy-start | bytes 393220
  7.2 143.7 %reduce-scatter.7.cloned.1.call-start = ((), (), s32[]{:S(2)}) async-start(), calls=%async_computation.3 | async-start | bytes 589824
  8.0 8.2 %collective-permute-start = (s32[97]{0:T(128)S(1)}, s32[97]{0:T(128)S(1)}, u32[]{:S(2)}, u32[]{:S(2)}) collective-permute-start(s32[97]{0:T(128)S(1)} %pad_add_fusion.1), channel_id=1, source_target_pairs={{0,1},{1,0},{2,3},{3,2},{4,5},{5,4},{6,7},{7,6},{8,9},{9,8},{10,11... | collective-permute-start | bytes 1172 | tf_op jit(solution)/shard_map/ppermute | solution.py:286
  8.5 8.3 %collective-permute-start.1 = (bf16[80,64,64]{0,2,1:T(8,128)(2,1)}, bf16[80,64,64]{0,2,1:T(8,128)(2,1)S(1)}, u32[]{:S(2)}, u32[]{:S(2)}) collective-permute-start(bf16[80,64,64]{0,2,1:T(8,128)(2,1)} %bitcast.35), channel_id=1, source_target_pairs={{0,1},{1,0},{2,3},{3,2},{4,5},{5,4},{6,7},{7,6},{8,9},{9,8},{10,11... | collective-permute-start | bytes 1966088 | tf_op jit(solution)/shard_map/ppermute | solution.py:285
  13.0 1.4 copy-start.1
  14.4 1.1 copy-start.3
  111.3 1.1 copy-start.2
  112.3 70.6 %copy-start.4 = (bf16[2,256,128]{2,1,0:T(8,128)(2,1)S(1)}, bf16[2,256,128]{2,1,0:T(8,128)(2,1)}, u32[]{:S(2)}) copy-start(bf16[2,256,128]{2,1,0:T(8,128)(2,1)} %get-tuple-element.5) | copy-start | bytes 393220
  112.3 70.6 %reduce-scatter.5.cloned.1.call-start = ((), (), s32[]{:S(2)}) async-start(), calls=%async_computation.2 | async-start | bytes 589824 | tf_op jit(solution)/shard_map/reduce_scatter | solution.py:319
  113.6 114.1 %all-reduce.3.cloned.1.call-start = ((), (), s32[]{:S(2)}) async-start(), calls=%async_computation.4 | async-start | bytes 655360 | tf_op jit(solution)/shard_map/psum | solution.py:328
Sparse Core Ops, SparseCore 0:
  112.5 38.4 reduce-scatter.6
  153.2 29.6 reduce-scatter.4
  185.9 41.7 all-reduce.2

commit v2 on v1

--- a/solution.py
+++ b/solution.py
@@ -80,9 +80,12 @@
 
 
 def power_kernel(
-    n_loop, n_chip, tele_ref, cot_ref, dense_ref, prop_ref, gt_ref,
-    tiles, zc, gr, ps, pr, qs, qr, prop_x, gt_x, prop_s, gt_s,
+    n_loop, n_chip, tele_ref, cot_ref, feats_ref, hidden_ref, slope_ref, second_ref, dense_ref,
+    prop_ref, first_out, second_out,
+    tiles, zc, gr, ps, pr, qs, qr, prop_x, gt, prop_s, gt_s,
+    f_s, f_x, f_h, f_p, f_q, f_r, f_g, s_s, s_x, s_h, s_p, s_q, s_r, s_g,
     tile_sem, ex_send, ex_recv, z_send, z_recv, g_send, g_recv, p_send, p_recv, q_send, q_recv,
+    pair_send, pair_recv, lane_send, lane_recv, chip_send, chip_recv, last_send, last_recv,
 ):
     l = lax.axis_index("loop")
     w = lax.axis_index("wide")
@@ -197,8 +200,9 @@
                 for step in range(1, STEPS):
                     kept = kept + gr[step, l, t].astype(jnp.float32)
                 gt_s[t] = (ALPHA * kept + gr[STEPS, l, t].astype(jnp.float32)).astype(jnp.bfloat16)
-            gt_copy = remote(gt_s.at[oc], gt_x, ex_send.at[3], ex_recv.at[3], partner)
+            gt_copy = remote(gt_s.at[oc], gt.at[c], ex_send.at[3], ex_recv.at[3], partner)
             gt_copy.start()
+            gt[c] = gt_s[c]
 
         for lp in loop_peers:
             p_copy(k, lp, l).wait_recv()
@@ -218,33 +222,126 @@
             prop_copy = remote(prop_s.at[oc], prop_x, ex_send.at[2], ex_recv.at[2], partner)
             prop_copy.start()
 
-    for k in range(STEPS):
-        for zp in chip_peers:
-            z_copy(k, z, zp).wait_send()
-            q_copy(k, z, zp).wait_send()
-        for lp in loop_peers:
-            g_copy(k, l, lp).wait_send()
-            p_copy(k, l, lp).wait_send()
     gt_copy.wait()
-    gt_ref[c] = gt_s[c]
-    gt_ref[oc] = gt_x[...]
+    grad_teleport = gt[...].reshape(2 * half, items)
+    contract_last = (((1,), (1,)), ((), ()))
+    second_sum = lax.dot_general(
+        hidden_ref[...], grad_teleport, contract_last, preferred_element_type=jnp.float32
+    )
+    rows_f, cols_f = f_s.shape[3], f_s.shape[4]
+    rows_s = s_s.shape[3]
+    for cc in range(2):
+        for lp in range(n_loop):
+            for zp in range(n_chip):
+                row = ((2 * zp + cc) * n_loop + lp) * rows_s
+                s_s[cc, lp, zp] = second_sum[row : row + rows_s].astype(jnp.bfloat16)
+
+    def pair_copy(which, src, dst):
+        return remote(src.at[oc], dst, pair_send.at[which], pair_recv.at[which], partner)
+
+    def lane_copy(which, src, dst, slot, target):
+        return remote(src.at[target], dst.at[slot], lane_send.at[which, target], lane_recv.at[which, slot], (target, w))
+
+    def chip_copy(which, src, dst, slot, target):
+        return remote(
+            src.at[target], dst.at[slot], chip_send.at[which, target], chip_recv.at[which, slot],
+            (l, 2 * target + c),
+        )
+
+    def last_copy(which, ref, slot, target):
+        return remote(ref.at[slot], ref.at[slot], last_send.at[which, target], last_recv.at[which, slot], (target, w))
+
+    pair_copy(1, s_s, s_x).start()
+    grad_hidden = jnp.dot(second_ref[...], grad_teleport, preferred_element_type=jnp.float32)
+    grad_pre = (grad_hidden * slope_ref[...]).astype(jnp.bfloat16)
+    first_sum = lax.dot_general(
+        feats_ref[...], grad_pre, contract_last, preferred_element_type=jnp.float32
+    )
+    for cc in range(2):
+        for lp in range(n_loop):
+            for zp in range(n_chip):
+                row = (2 * zp + cc) * rows_f
+                f_s[cc, lp, zp] = first_sum[
+                    row : row + rows_f, lp * cols_f : (lp + 1) * cols_f
+                ].astype(jnp.bfloat16)
+    pair_copy(0, f_s, f_x).start()
+    sets = (
+        (1, s_s, s_x, s_h, s_p, s_q, s_r, s_g),
+        (0, f_s, f_x, f_h, f_p, f_q, f_r, f_g),
+    )
+    wide = jnp.float32
+    for which, own, got, sums, _p, _q, _r, _g in sets:
+        pair_copy(which, own, got).wait()
+        for lp in loop_peers:
+            sums[lp] = (own[c, lp].astype(wide) + got[lp].astype(wide)).astype(jnp.bfloat16)
+            lane_copy(which, sums, _p, l, lp).start()
+    for which, own, got, sums, parts, quarter, _r, _g in sets:
+        total = own[c, l].astype(wide) + got[l].astype(wide)
+        for lp in loop_peers:
+            lane_copy(which, sums, parts, lp, l).wait_recv()
+            total = total + parts[lp].astype(wide)
+        quarter[...] = total.astype(jnp.bfloat16)
+        for zp in chip_peers:
+            chip_copy(which, quarter, _r, z, zp).start()
+    for which, _o, _x, _h, _p, quarter, pieces, final in sets:
+        total = quarter[z].astype(wide)
+        for zp in chip_peers:
+            chip_copy(which, quarter, pieces, zp, z).wait_recv()
+            total = total + pieces[zp].astype(wide)
+        final[l] = total.astype(jnp.bfloat16)
+        for lp in loop_peers:
+            last_copy(which, final, l, lp).start()
     prop_copy.wait()
     prop_ref[c] = prop_s[c]
     prop_ref[oc] = prop_x[...]
-
-
-def power_steps(tele, cot, dense, n_loop, n_chip):
+    for k in range(STEPS):
+        for zp in chip_peers:
+            z_copy(k, z, zp).wait_send()
+            q_copy(k, z, zp).wait_send()
+        for lp in loop_peers:
+            g_copy(k, l, lp).wait_send()
+            p_copy(k, l, lp).wait_send()
+    for which, _o, _x, sums, parts, quarter, pieces, final in sets:
+        for lp in loop_peers:
+            lane_copy(which, sums, parts, l, lp).wait_send()
+            last_copy(which, final, l, lp).wait_send()
+        for zp in chip_peers:
+            chip_copy(which, quarter, pieces, z, zp).wait_send()
+        for lp in loop_peers:
+            last_copy(which, final, lp, l).wait_recv()
+    for lp in range(n_loop):
+        first_out[:, lp * cols_f : (lp + 1) * cols_f] = f_g[lp].astype(wide)
+        second_out[lp * rows_s : (lp + 1) * rows_s, :] = s_g[lp].astype(wide)
+
+
+def sum_buffers(n_loop, n_chip, rows, cols):
+    shapes = (
+        (2, n_loop, n_chip, rows, cols),
+        (n_loop, n_chip, rows, cols),
+        (n_loop, n_chip, rows, cols),
+        (n_loop, n_chip, rows, cols),
+        (n_chip, rows, cols),
+        (n_chip, rows, cols),
+        (n_loop, rows, cols),
+    )
+    return [pltpu.VMEM(shape, jnp.bfloat16) for shape in shapes]
+
+
+def power_steps(tele, cot, feats, hidden, slope, second, dense, n_loop, n_chip):
     _, items, half = tele.shape
+    features, units = feats.shape[0], hidden.shape[0]
+    first_rows, second_rows = features // (2 * n_chip), units // (2 * n_chip)
     bf16, dma = jnp.bfloat16, pltpu.SemaphoreType.DMA
     vmem = pl.BlockSpec(memory_space=pltpu.VMEM)
     return pl.pallas_call(
         functools.partial(power_kernel, n_loop, n_chip),
         out_shape=(
             jax.ShapeDtypeStruct((2, items, half), bf16),
-            jax.ShapeDtypeStruct((2, half, items), bf16),
+            jax.ShapeDtypeStruct((first_rows, units), jnp.float32),
+            jax.ShapeDtypeStruct((second_rows, features), jnp.float32),
         ),
-        in_specs=[vmem, vmem, pl.BlockSpec(memory_space=pl.ANY)],
-        out_specs=(vmem, vmem),
+        in_specs=[vmem] * 6 + [pl.BlockSpec(memory_space=pl.ANY)],
+        out_specs=(vmem, vmem, vmem),
         scratch_shapes=[
             pltpu.VMEM(dense.shape, bf16),
             pltpu.VMEM((STEPS, n_chip, 2, items, half), bf16),
@@ -254,9 +351,11 @@
             pltpu.VMEM((STEPS, n_chip, 2, half, items), bf16),
             pltpu.VMEM((STEPS, n_chip, 2, half, items), bf16),
             pltpu.VMEM((items, half), bf16),
-            pltpu.VMEM((half, items), bf16),
+            pltpu.VMEM((2, half, items), bf16),
             pltpu.VMEM((2, items, half), bf16),
             pltpu.VMEM((2, half, items), bf16),
+            *sum_buffers(n_loop, n_chip, first_rows, units // n_loop),
+            *sum_buffers(n_loop, n_chip, second_rows // n_loop, features),
             dma,
             dma((4,)),
             dma((4,)),
@@ -268,12 +367,20 @@
             dma((STEPS, n_loop)),
             dma((STEPS, n_chip)),
             dma((STEPS, n_chip)),
+            dma((2,)),
+            dma((2,)),
+            dma((2, n_loop)),
+            dma((2, n_loop)),
+            dma((2, n_chip)),
+            dma((2, n_chip)),
+            dma((2, n_loop)),
+            dma((2, n_loop)),
         ],
         compiler_params=pltpu.CompilerParams(
-            collective_id=0, has_side_effects=True, vmem_limit_bytes=60 * 2**20
+            collective_id=0, has_side_effects=True, vmem_limit_bytes=63 * 2**20
         ),
         name="power_steps",
-    )(tele, cot, dense)
+    )(tele, cot, feats, hidden, slope, second, dense)
 
 
 def body(feats, w_first, w_second, cotangent, block_values, row_ptr, col_idx):
@@ -287,47 +394,29 @@
     flat_feats = feats[0]
     items, features = flat_feats.shape
     half = features // 2
-    pre_act = jnp.dot(flat_feats, w_first, preferred_element_type=jnp.float32)
+    pre_act = lax.dot_general(
+        w_first, flat_feats, (((0,), (1,)), ((), ())), preferred_element_type=jnp.float32
+    )
     hidden = jax.nn.silu(pre_act).astype(jnp.bfloat16)
-    teleport = jnp.dot(hidden, w_second, preferred_element_type=jnp.float32).astype(jnp.bfloat16)
+    teleport = lax.dot_general(
+        hidden, w_second, (((0,), (0,)), ((), ())), preferred_element_type=jnp.float32
+    ).astype(jnp.bfloat16)
     core = lax.rem(lax.axis_index("wide"), 2).astype(jnp.int32).reshape(1)
     dense = dense_pair(
         jnp.stack([index, other_index]), core, mine, other, n_loop, n_chip, items
     )
-    prop_halves, gt_flipped = power_steps(
+    prop_halves, grad_first, grad_second = power_steps(
         teleport.reshape(items, 2, half).transpose(1, 0, 2),
         cotangent[0].T.reshape(2, half, items),
+        flat_feats.T,
+        hidden,
+        silu_slope(pre_act),
+        w_second,
         dense,
         n_loop,
         n_chip,
     )
     current = prop_halves.transpose(1, 0, 2).reshape(items, features)
-    grad_teleport = gt_flipped.reshape(features, items).T
-    grad_hidden = lax.dot_general(
-        grad_teleport, w_second, (((1,), (1,)), ((), ())), preferred_element_type=jnp.float32
-    )
-    grad_pre = (grad_hidden * silu_slope(pre_act)).astype(jnp.bfloat16)
-    contract_items = (((0,), (0,)), ((), ()))
-    first_part = lax.psum_scatter(
-        lax.dot_general(
-            flat_feats, grad_pre, contract_items, preferred_element_type=jnp.float32
-        ).astype(jnp.bfloat16),
-        "wide",
-        scatter_dimension=0,
-        tiled=True,
-    )
-    second_part = lax.psum_scatter(
-        lax.dot_general(
-            hidden, grad_teleport, contract_items, preferred_element_type=jnp.float32
-        ).astype(jnp.bfloat16),
-        "wide",
-        scatter_dimension=0,
-        tiled=True,
-    )
-    grad_first, grad_second = (
-        lax.psum(first_part, "loop").astype(jnp.float32),
-        lax.psum(second_part, "loop").astype(jnp.float32),
-    )
     return (current[None], grad_first, grad_second)
 
 

time: 239 us -> 135 us (0.56)
  waiting for transfers between devices: 111 us -> 0.01 us
  Pallas kernels: 89.7 us -> 115 us
  between operations: 13.8 us -> 0.68 us
  matrix products: 4.89 us -> 1.99 us
    psum x1 -> x0, waiting for transfers between devices: 43.8 us -> none  [body(): lax.psum(first_part, 'loop').astype(jnp.float32)]
    unnamed x4 -> x0, waiting for transfers between devices: 37.3 us -> none
    reduce_scatter x1 -> x0, waiting for transfers between devices: 30.3 us -> none  [body(): lax.psum_scatter(lax.dot_general(hidden, grad_teleport, contract_items, p...]
    pallas_call x1, Pallas kernels: 79.6 us -> 105 us  [power_steps(): pl.pallas_call(functools.partial(power_kernel, n_loop, n_chip), out_shape...]
    dot_general x4 -> x2, matrix products: 4.89 us -> 1.99 us  [the longest x1 1.64 us: body(): lax.dot_general(w_first, flat_feats, (((0,), (1,)), ((), ())), preferred_...]
    unnamed x17 -> x15, local copies, waits for them, and re-layouts: 8.88 us -> 9.16 us
  transfers between devices with their start and end apart: 5 -> 2, of which waited for: 3 -> 0; matrix products, arithmetic and copies ran while one was open for 5% -> 7% of each run, Pallas kernels for 0% -> 0%
where the time goes in v2:
time: 135 us
  Pallas kernels  115 us (85%)
  local copies, waits for them, and re-layouts  14.4 us (11%)
  other arithmetic  2.11 us (2%)
  matrix products  1.99 us (1%)
    pallas_call x1, Pallas kernels, power_steps(): pl.pallas_call(functools.partial(power_kernel, n_loop, n_chip), out_shape...  105 us
    pallas_call x1, Pallas kernels, dense_pair(): pl.pallas_call(dense_kernel, out_shape=jax.ShapeDtypeStruct((n_loop, n_ch...  10.4 us
    unnamed x15, local copies, waits for them, and re-layouts  9.16 us
    ppermute x1, local copies, waits for them, and re-layouts, body(): other = lax.ppermute(mine, 'wide', swap)  2.73 us
  transfers between devices with their start and end apart: 2, of which 0 were waited for; matrix products, arithmetic and copies ran while one was open for 7% of the time, Pallas kernels for 0%

profile of v2, /device:TPU:0, one launch (start us, length us, event | category | flops | bytes accessed | tf_op | source)
XLA Modules:
  0.0 134.7 jit_solution(15255884608026453417)
XLA Ops:
  0.6 0.0 copy-start
  0.6 0.0 copy-start.3
  0.7 0.8 pad_add_fusion.1
  1.5 0.5 collective-permute-start
  2.0 0.1 collective-permute-start.1
  2.0 0.7 fusion.5
  2.8 3.7 %copy.22 = bf16[1,1,80,64,64]{4,3,2,1,0:T(8,128)(2,1)} copy(bf16[1,1,80,64,64]{2,4,3,1,0:T(8,128)(2,1)} %param.11) | data formatting | bytes 1310720 | tf_op args[4]
  6.5 0.0 copy-done.3
  6.5 0.8 copy.19
  7.2 0.0 copy-done
  7.2 0.0 copy-start.1
  7.2 1.6 %add_multiply_fusion = (f32[1024,256]{1,0:T(8,128)}, bf16[1024,256]{1,0:T(8,128)(2,1)S(1)}) fusion(bf16[256,1024]{1,0:T(8,128)(2,1)S(1)} %copy-done, bf16[1,256,256]{2,1,0:T(8,128)(2,1)S(1)} %copy-done.3), kind=kOutput, calls=%fused_computation.1 | convolution fusion | flops 136577024 | bytes 2228224 | tf_op jit(solution)/shard_map/dot_general | solution.py:397
  8.9 0.0 copy-start.2
  8.9 0.0 copy-start.4
  8.9 0.8 copy-done.2
  9.7 0.0 copy-done.1
  9.7 0.4 convolution_convert_fusion
  10.0 0.8 copy.20
  10.8 0.0 copy-done.4
  10.8 0.8 copy.21
  11.6 0.0 collective-permute-done
  11.6 0.5 pad_add_fusion.index_ref
  12.1 0.0 collective-permute-done.1
  12.1 2.7 %copy.24.other_ref = bf16[80,64,64]{2,1,0:T(8,128)(2,1)} copy(bf16[80,64,64]{0,2,1:T(8,128)(2,1)S(1)} %collective-permute-done.1) | data formatting | bytes 1310720 | tf_op jit(solution)/shard_map/ppermute | solution.py:392
  14.8 10.4 %dense_pair.1.dense_ref = bf16[4,4,2,256,512]{4,3,2,1,0:T(8,128)(2,1)} custom-call(s32[2,97]{1,0:T(2,128)} %pad_add_fusion.index_ref, s32[1]{0:T(128)} %bitcast.11.core_ref, bf16[80,64,64]{2,1,0:T(8,128)(2,1)} %bitcast.27, bf16[80,64,64]{2,1,0:T(8,128)(2,1)} %copy.24.other_ref), custom_call_target="tpu_custom_call" | custom-call | tf_op jit(solution)/shard_map/dense_pair/pallas_call | solution.py:65
  25.3 104.5 %power_steps.1 = (bf16[2,256,128]{2,1,0:T(8,128)(2,1)}, f32[32,1024]{1,0:T(8,128)}, f32[128,256]{1,0:T(8,128)}) custom-call(bf16[2,256,128]{2,1,0:T(8,128)(2,1)} %bitcast.30, bf16[2,128,256]{2,1,0:T(8,128)(2,1)} %bitcast.31, bf16[256,256]{1,0:T(8,128)(2,1)} %bitcast.29, bf16[1024,256]{1,0:T(8,128)(2,1)} %copy-done.2, ...), custom_call_target="tpu_custom_call" | custom-call | tf_op jit(solution)/shard_map/power_steps/pallas_call | solution.py:336
  129.8 1.0 copy.25
  130.8 0.8 copy.26
  131.6 1.6 %copy.30 = f32[32,1024]{1,0:T(8,128)} copy(f32[32,1024]{1,0:T(8,128)} %get-tuple-element.21) | data formatting | bytes 262144
  133.2 1.6 %copy.31 = f32[128,256]{1,0:T(8,128)} copy(f32[128,256]{1,0:T(8,128)} %get-tuple-element.22) | data formatting | bytes 262144
Async XLA Ops:
  0.6 6.6 %copy-start = (bf16[256,1024]{1,0:T(8,128)(2,1)S(1)}, bf16[256,1024]{1,0:T(8,128)(2,1)}, u32[]{:S(2)}) copy-start(bf16[256,1024]{1,0:T(8,128)(2,1)} %param.8) | copy-start | bytes 1572868
  0.6 5.8 %copy-start.3 = (bf16[1,256,256]{2,1,0:T(8,128)(2,1)S(1)}, bf16[1,256,256]{2,1,0:T(8,128)(2,1)}, u32[]{:S(2)}) copy-start(bf16[1,256,256]{2,1,0:T(8,128)(2,1)} %param.7) | copy-start | bytes 393220
  1.5 10.1 %collective-permute-start = (s32[97]{0:T(128)S(1)}, s32[97]{0:T(128)S(1)}, u32[]{:S(2)}, u32[]{:S(2)}) collective-permute-start(s32[97]{0:T(128)S(1)} %pad_add_fusion.1), channel_id=1, source_target_pairs={{0,1},{1,0},{2,3},{3,2},{4,5},{5,4},{6,7},{7,6},{8,9},{9,8},{10,11... | collective-permute-start | bytes 1172 | tf_op jit(solution)/shard_map/ppermute | solution.py:393
  2.0 10.1 %collective-permute-start.1 = (bf16[80,64,64]{0,2,1:T(8,128)(2,1)}, bf16[80,64,64]{0,2,1:T(8,128)(2,1)S(1)}, u32[]{:S(2)}, u32[]{:S(2)}) collective-permute-start(bf16[80,64,64]{0,2,1:T(8,128)(2,1)} %bitcast.28), channel_id=1, source_target_pairs={{0,1},{1,0},{2,3},{3,2},{4,5},{5,4},{6,7},{7,6},{8,9},{9,8},{10,11... | collective-permute-start | bytes 1966088 | tf_op jit(solution)/shard_map/ppermute | solution.py:392
  7.2 2.4 %copy-start.1 = (bf16[1024,256]{1,0:T(8,128)(2,1)S(1)}, bf16[1024,256]{1,0:T(8,128)(2,1)}, u32[]{:S(2)}) copy-start(bf16[1024,256]{1,0:T(8,128)(2,1)} %second_ref.1) | copy-start | bytes 1572868
  8.9 0.8 copy-start.2
  8.9 1.9 %copy-start.4 = (bf16[1,256,256]{2,1,0:T(8,128)(2,1)S(1)}, bf16[1,256,256]{2,1,0:T(8,128)(2,1)}, u32[]{:S(2)}) copy-start(bf16[1,256,256]{2,1,0:T(8,128)(2,1)} %param.10) | copy-start | bytes 393220

commit v3 on v2

--- a/solution.py
+++ b/solution.py
@@ -82,7 +82,7 @@
 def power_kernel(
     n_loop, n_chip, tele_ref, cot_ref, feats_ref, hidden_ref, slope_ref, second_ref, dense_ref,
     prop_ref, first_out, second_out,
-    tiles, zc, gr, ps, pr, qs, qr, prop_x, gt, prop_s, gt_s,
+    tiles, zc, gr, ps, pr, qs, qr, own_q, prop_x, gt, prop_s, gt_s,
     f_s, f_x, f_h, f_p, f_q, f_r, f_g, s_s, s_x, s_h, s_p, s_q, s_r, s_g,
     tile_sem, ex_send, ex_recv, z_send, z_recv, g_send, g_recv, p_send, p_recv, q_send, q_recv,
     pair_send, pair_recv, lane_send, lane_recv, chip_send, chip_recv, last_send, last_recv,
@@ -112,8 +112,39 @@
             device_id=target, device_id_type=MESH,
         )
 
-    def z_copy(k, slot, target):
-        return remote(zc.at[k, slot], zc.at[k, slot], z_send.at[k, target], z_recv.at[k, slot], (l, 2 * target + c))
+    def z_copy(k, slot, t, way):
+        target = z + 1 - 2 * way
+        return remote(
+            zc.at[k, slot, t], zc.at[k, slot, t], z_send.at[k, way, slot, t], z_recv.at[k, slot, t],
+            (l, 2 * target + c),
+        )
+
+    def z_pass(k, slot, held):
+        if not held:
+            for t in range(2):
+                for way, inside in ((0, z < n_chip - 1), (1, z > 0)):
+                    pl.when(inside)(lambda t=t, way=way: z_copy(k, slot, t, way).start())
+            return
+        left, right = z - held, z + held
+        for t in range(2):
+
+            @pl.when(left >= 0)
+            def _():
+                z_copy(k, left, t, 0).wait_recv()
+                pl.when(z < n_chip - 1)(lambda: z_copy(k, left, t, 0).start())
+
+            @pl.when(right < n_chip)
+            def _():
+                z_copy(k, right, t, 1).wait_recv()
+                pl.when(z > 0)(lambda: z_copy(k, right, t, 1).start())
+
+    def z_sent(k):
+        for t in range(2):
+            for slot in range(n_chip):
+                pl.when((z >= slot) & (z < n_chip - 1))(
+                    lambda: z_copy(k, slot, t, 0).wait_send()
+                )
+                pl.when((z <= slot) & (z > 0))(lambda: z_copy(k, slot, t, 1).wait_send())
 
     def g_copy(k, slot, target):
         return remote(gr.at[k, slot], gr.at[k, slot], g_send.at[k, target], g_recv.at[k, slot], (target, w))
@@ -121,8 +152,27 @@
     def p_copy(k, slot, target):
         return remote(ps.at[k, target], pr.at[k, slot], p_send.at[k, target], p_recv.at[k, slot], (target, w))
 
-    def q_copy(k, slot, target):
-        return remote(qs.at[k, target], qr.at[k, slot], q_send.at[k, target], q_recv.at[k, slot], (l, 2 * target + c))
+    def q_copy(k, dest, t, way):
+        target = z + 1 - 2 * way
+        return remote(
+            qs.at[k, dest, t], qr.at[k, way, dest, t], q_send.at[k, dest, t], q_recv.at[k, way, dest, t],
+            (l, 2 * target + c),
+        )
+
+    def q_add(k, dest, way):
+        for t in range(2):
+            q_copy(k, dest, t, way).wait_recv()
+            total = qs[k, dest, t].astype(jnp.float32) + qr[k, way, dest, t].astype(jnp.float32)
+            qs[k, dest, t] = total.astype(jnp.bfloat16)
+            q_copy(k, dest, t, way).start()
+
+    def q_stage(k, j):
+        up, down = n_chip - 1 - j, j
+        upper = z >= n_chip // 2
+        goes_down = (z < n_chip - 1) & (z > down)
+        pl.when(goes_down & upper)(lambda: q_add(k, down, 1))
+        pl.when((z > 0) & (z < up))(lambda: q_add(k, up, 0))
+        pl.when(goes_down & (z < n_chip // 2))(lambda: q_add(k, down, 1))
 
     cot_x = remote(cot_ref.at[oc], gr.at[0, l, c], ex_send.at[1], ex_recv.at[1], partner)
     cot_x.start()
@@ -134,8 +184,7 @@
     for lp in loop_peers:
         g_copy(0, l, lp).start()
     tele_x.wait()
-    for zp in chip_peers:
-        z_copy(0, z, zp).start()
+    z_pass(0, z, 0)
     load.wait()
 
     def forward_part(k, lp):
@@ -158,22 +207,33 @@
         return total
 
     for k in range(STEPS):
+        if n_chip > 1:
+            z_pass(k, z, 1)
         for lp in loop_peers:
             g_copy(k, lp, l).wait_recv()
 
         def q_step(j, carry):
-            zp = lax.rem(z + 1 + j, n_chip)
-            value = adjoint_part(k, zp).astype(jnp.bfloat16)
-            for t in range(2):
-                qs[k, zp, t] = value[:, t * items : (t + 1) * items]
-            q_copy(k, z, zp).start()
+            flip = (2 * z) // n_chip
+            zp = (1 - flip) * (n_chip - 1 - j) + flip * j
+
+            @pl.when(zp != z)
+            def _():
+                value = adjoint_part(k, zp).astype(jnp.bfloat16)
+                for t in range(2):
+                    qs[k, zp, t] = value[:, t * items : (t + 1) * items]
+                for t in range(2):
+                    pl.when(z == 0)(lambda: q_copy(k, zp, t, 0).start())
+                    pl.when(z == n_chip - 1)(lambda: q_copy(k, zp, t, 1).start())
+
             return carry
 
-        lax.fori_loop(0, n_chip - 1, q_step, 0)
-        own_q = adjoint_part(k, z)
-
-        for zp in chip_peers:
-            z_copy(k, zp, z).wait_recv()
+        lax.fori_loop(0, n_chip, q_step, 0)
+        own_q[...] = adjoint_part(k, z)
+        for held in range(2, n_chip - 1):
+            z_pass(k, z, held)
+        q_stage(k, 0)
+        if n_chip > 2:
+            z_pass(k, z, n_chip - 1)
 
         def p_step(j, carry):
             lp = lax.rem(l + 1 + j, n_loop)
@@ -184,13 +244,18 @@
         lax.fori_loop(0, n_loop - 1, p_step, 0)
         own_p = forward_part(k, l)
 
-        for zp in chip_peers:
-            q_copy(k, zp, z).wait_recv()
+        for j in range(1, n_chip - 1):
+            q_stage(k, j)
         for t in range(2):
-            total = own_q[:, t * items : (t + 1) * items]
-            for zp in chip_peers:
-                total = total + qr[k, zp, t].astype(jnp.float32)
-            gr[k + 1, l, t] = ((1.0 - ALPHA) * total).astype(jnp.bfloat16)
+            lanes = slice(t * items, (t + 1) * items)
+            for way, inside in ((0, z > 0), (1, z < n_chip - 1)):
+
+                @pl.when(inside)
+                def _():
+                    q_copy(k, z, t, way).wait_recv()
+                    own_q[:, lanes] = own_q[:, lanes] + qr[k, way, z, t].astype(jnp.float32)
+
+            gr[k + 1, l, t] = ((1.0 - ALPHA) * own_q[:, lanes]).astype(jnp.bfloat16)
         if k < STEPS - 1:
             for lp in loop_peers:
                 g_copy(k + 1, l, lp).start()
@@ -214,8 +279,7 @@
         if k < STEPS - 1:
             for t in range(2):
                 zc[k + 1, z, t] = mixed[t * items : (t + 1) * items]
-            for zp in chip_peers:
-                z_copy(k + 1, z, zp).start()
+            z_pass(k + 1, z, 0)
         else:
             for t in range(2):
                 prop_s[t] = mixed[t * items : (t + 1) * items]
@@ -295,9 +359,11 @@
     prop_ref[c] = prop_s[c]
     prop_ref[oc] = prop_x[...]
     for k in range(STEPS):
-        for zp in chip_peers:
-            z_copy(k, z, zp).wait_send()
-            q_copy(k, z, zp).wait_send()
+        z_sent(k)
+        for t in range(2):
+            for dest in range(n_chip):
+                pl.when(z < dest)(lambda: q_copy(k, dest, t, 0).wait_send())
+                pl.when(z > dest)(lambda: q_copy(k, dest, t, 1).wait_send())
         for lp in loop_peers:
             g_copy(k, l, lp).wait_send()
             p_copy(k, l, lp).wait_send()
@@ -349,7 +415,8 @@
             pltpu.VMEM((STEPS, n_loop, 2 * items, half), bf16),
             pltpu.VMEM((STEPS, n_loop, 2 * items, half), bf16),
             pltpu.VMEM((STEPS, n_chip, 2, half, items), bf16),
-            pltpu.VMEM((STEPS, n_chip, 2, half, items), bf16),
+            pltpu.VMEM((STEPS, 2, n_chip, 2, half, items), bf16),
+            pltpu.VMEM((half, 2 * items), jnp.float32),
             pltpu.VMEM((items, half), bf16),
             pltpu.VMEM((2, half, items), bf16),
             pltpu.VMEM((2, items, half), bf16),
@@ -359,14 +426,14 @@
             dma,
             dma((4,)),
             dma((4,)),
-            dma((STEPS, n_chip)),
-            dma((STEPS, n_chip)),
+            dma((STEPS, 2, n_chip, 2)),
+            dma((STEPS, n_chip, 2)),
             dma((STEPS, n_loop)),
             dma((STEPS, n_loop)),
             dma((STEPS, n_loop)),
             dma((STEPS, n_loop)),
-            dma((STEPS, n_chip)),
-            dma((STEPS, n_chip)),
+            dma((STEPS, n_chip, 2)),
+            dma((STEPS, 2, n_chip, 2)),
             dma((2,)),
             dma((2,)),
             dma((2, n_loop)),

time: 135 us -> 130 us (0.963)
  Pallas kernels: 115 us -> 110 us
    pallas_call x1, Pallas kernels: 105 us -> 97.9 us  [power_steps(): pl.pallas_call(functools.partial(power_kernel, n_loop, n_chip), out_shape...]
where the time goes in v3:
time: 130 us; the launch traced here: 129 us
  Pallas kernels  110 us (85%)
  local copies, waits for them, and re-layouts  14.4 us (11%)
  other arithmetic  2.11 us (2%)
  matrix products  1.99 us (2%)
    pallas_call x1, Pallas kernels, power_steps(): pl.pallas_call(functools.partial(power_kernel, n_loop, n_chip), out_shape...  97.9 us
    pallas_call x1, Pallas kernels, dense_pair(): pl.pallas_call(dense_kernel, out_shape=jax.ShapeDtypeStruct((n_loop, n_ch...  11.6 us
    unnamed x15, local copies, waits for them, and re-layouts  9.16 us
    ppermute x1, local copies, waits for them, and re-layouts, body(): other = lax.ppermute(mine, 'wide', swap)  2.73 us
  transfers between devices with their start and end apart: 2, of which 0 were waited for; matrix products, arithmetic and copies ran while one was open for 7% of the time, Pallas kernels for 0%

profile of v3, /device:TPU:0, one launch (start us, length us, event | category | flops | bytes accessed | tf_op | source)
XLA Modules:
  0.0 129.3 jit_solution(1848297663176496423)
XLA Ops:
  0.6 0.0 copy-start
  0.6 0.0 copy-start.3
  0.7 0.8 pad_add_fusion.1
  1.5 0.5 collective-permute-start
  2.0 0.1 collective-permute-start.1
  2.0 0.7 fusion.5
  2.8 3.7 %copy.22 = bf16[1,1,80,64,64]{4,3,2,1,0:T(8,128)(2,1)} copy(bf16[1,1,80,64,64]{2,4,3,1,0:T(8,128)(2,1)} %param.11) | data formatting | bytes 1310720 | tf_op args[4]
  6.5 0.0 copy-done.3
  6.5 0.8 copy.19
  7.2 0.0 copy-done
  7.2 0.0 copy-start.1
  7.2 1.6 %add_multiply_fusion = (f32[1024,256]{1,0:T(8,128)}, bf16[1024,256]{1,0:T(8,128)(2,1)S(1)}) fusion(bf16[256,1024]{1,0:T(8,128)(2,1)S(1)} %copy-done, bf16[1,256,256]{2,1,0:T(8,128)(2,1)S(1)} %copy-done.3), kind=kOutput, calls=%fused_computation.1 | convolution fusion | flops 136577024 | bytes 2228224 | tf_op jit(solution)/shard_map/dot_general | solution.py:464
  8.9 0.0 copy-start.2
  8.9 0.0 copy-start.4
  8.9 0.8 copy-done.2
  9.7 0.0 copy-done.1
  9.7 0.4 convolution_convert_fusion
  10.0 0.8 copy.20
  10.8 0.0 copy-done.4
  10.8 0.8 copy.21
  11.6 0.0 collective-permute-done
  11.6 0.5 pad_add_fusion.index_ref
  12.1 0.0 collective-permute-done.1
  12.1 2.7 %copy.24.other_ref = bf16[80,64,64]{2,1,0:T(8,128)(2,1)} copy(bf16[80,64,64]{0,2,1:T(8,128)(2,1)S(1)} %collective-permute-done.1) | data formatting | bytes 1310720 | tf_op jit(solution)/shard_map/ppermute | solution.py:459
  14.8 11.6 %dense_pair.1.dense_ref = bf16[4,4,2,256,512]{4,3,2,1,0:T(8,128)(2,1)} custom-call(s32[2,97]{1,0:T(2,128)} %pad_add_fusion.index_ref, s32[1]{0:T(128)} %bitcast.11.core_ref, bf16[80,64,64]{2,1,0:T(8,128)(2,1)} %bitcast.27, bf16[80,64,64]{2,1,0:T(8,128)(2,1)} %copy.24.other_ref), custom_call_target="tpu_custom_call" | custom-call | tf_op jit(solution)/shard_map/dense_pair/pallas_call | solution.py:65
  26.5 97.9 %power_steps.1 = (bf16[2,256,128]{2,1,0:T(8,128)(2,1)}, f32[32,1024]{1,0:T(8,128)}, f32[128,256]{1,0:T(8,128)}) custom-call(bf16[2,256,128]{2,1,0:T(8,128)(2,1)} %bitcast.30, bf16[2,128,256]{2,1,0:T(8,128)(2,1)} %bitcast.31, bf16[256,256]{1,0:T(8,128)(2,1)} %bitcast.29, bf16[1024,256]{1,0:T(8,128)(2,1)} %copy-done.2, ...), custom_call_target="tpu_custom_call" | custom-call | tf_op jit(solution)/shard_map/power_steps/pallas_call | solution.py:402
  124.4 1.0 copy.25
  125.4 0.8 copy.26
  126.2 1.6 %copy.30 = f32[32,1024]{1,0:T(8,128)} copy(f32[32,1024]{1,0:T(8,128)} %get-tuple-element.21) | data formatting | bytes 262144
  127.7 1.6 %copy.31 = f32[128,256]{1,0:T(8,128)} copy(f32[128,256]{1,0:T(8,128)} %get-tuple-element.22) | data formatting | bytes 262144
Async XLA Ops:
  0.6 6.6 %copy-start = (bf16[256,1024]{1,0:T(8,128)(2,1)S(1)}, bf16[256,1024]{1,0:T(8,128)(2,1)}, u32[]{:S(2)}) copy-start(bf16[256,1024]{1,0:T(8,128)(2,1)} %param.8) | copy-start | bytes 1572868
  0.6 5.8 %copy-start.3 = (bf16[1,256,256]{2,1,0:T(8,128)(2,1)S(1)}, bf16[1,256,256]{2,1,0:T(8,128)(2,1)}, u32[]{:S(2)}) copy-start(bf16[1,256,256]{2,1,0:T(8,128)(2,1)} %param.7) | copy-start | bytes 393220
  1.5 10.1 %collective-permute-start = (s32[97]{0:T(128)S(1)}, s32[97]{0:T(128)S(1)}, u32[]{:S(2)}, u32[]{:S(2)}) collective-permute-start(s32[97]{0:T(128)S(1)} %pad_add_fusion.1), channel_id=1, source_target_pairs={{0,1},{1,0},{2,3},{3,2},{4,5},{5,4},{6,7},{7,6},{8,9},{9,8},{10,11... | collective-permute-start | bytes 1172 | tf_op jit(solution)/shard_map/ppermute | solution.py:460
  2.0 10.1 %collective-permute-start.1 = (bf16[80,64,64]{0,2,1:T(8,128)(2,1)}, bf16[80,64,64]{0,2,1:T(8,128)(2,1)S(1)}, u32[]{:S(2)}, u32[]{:S(2)}) collective-permute-start(bf16[80,64,64]{0,2,1:T(8,128)(2,1)} %bitcast.28), channel_id=1, source_target_pairs={{0,1},{1,0},{2,3},{3,2},{4,5},{5,4},{6,7},{7,6},{8,9},{9,8},{10,11... | collective-permute-start | bytes 1966088 | tf_op jit(solution)/shard_map/ppermute | solution.py:459
  7.2 2.4 %copy-start.1 = (bf16[1024,256]{1,0:T(8,128)(2,1)S(1)}, bf16[1024,256]{1,0:T(8,128)(2,1)}, u32[]{:S(2)}) copy-start(bf16[1024,256]{1,0:T(8,128)(2,1)} %second_ref.1) | copy-start | bytes 1572868
  8.9 0.8 copy-start.2
  8.9 1.9 %copy-start.4 = (bf16[1,256,256]{2,1,0:T(8,128)(2,1)S(1)}, bf16[1,256,256]{2,1,0:T(8,128)(2,1)}, u32[]{:S(2)}) copy-start(bf16[1,256,256]{2,1,0:T(8,128)(2,1)} %param.10) | copy-start | bytes 393220

commit v4 on v3

--- a/solution.py
+++ b/solution.py
@@ -35,15 +35,21 @@
             first = index_ref[tile, strip * per_strip + row]
             last = index_ref[tile, strip * per_strip + row + 1]
 
-            def add(slot, carry):
-                col = index_ref[tile, pointers + slot]
-                block = values_ref[slot].astype(jnp.float32)
-                wide = jnp.concatenate([block, block], axis=1)
-                wide = jnp.where(upper == col % 2, wide, 0.0)
-                acc[col // 2] = acc[col // 2] + wide
+            def add(pair, carry):
+                slot = first + 2 * pair
+                after = jnp.minimum(slot + 1, last - 1)
+                cols = (index_ref[tile, pointers + slot], index_ref[tile, pointers + after])
+                sides = (cols[0] % 2, jnp.where(slot + 1 < last, cols[1] % 2, 2))
+                blocks = (values_ref[slot].astype(jnp.float32), values_ref[after].astype(jnp.float32))
+                wides = [
+                    jnp.where(upper == side, jnp.concatenate([block, block], axis=1), 0.0)
+                    for side, block in zip(sides, blocks)
+                ]
+                for col, wide in zip(cols, wides):
+                    acc[col // 2] = acc[col // 2] + wide
                 return carry
 
-            lax.fori_loop(first, last, add, 0)
+            lax.fori_loop(0, (last - first + 1) // 2, add, 0)
             for chip in range(chips):
                 for part in range(per_chip):
                     out_ref[
@@ -356,8 +362,13 @@
         for lp in loop_peers:
             last_copy(which, final, l, lp).start()
     prop_copy.wait()
-    prop_ref[c] = prop_s[c]
-    prop_ref[oc] = prop_x[...]
+    for side in range(2):
+
+        @pl.when(c == side)
+        def _():
+            prop_ref[:, side * half : (side + 1) * half] = prop_s[side]
+            prop_ref[:, (1 - side) * half : (2 - side) * half] = prop_x[...]
+
     for k in range(STEPS):
         z_sent(k)
         for t in range(2):
@@ -376,8 +387,8 @@
         for lp in loop_peers:
             last_copy(which, final, lp, l).wait_recv()
     for lp in range(n_loop):
-        first_out[:, lp * cols_f : (lp + 1) * cols_f] = f_g[lp].astype(wide)
-        second_out[lp * rows_s : (lp + 1) * rows_s, :] = s_g[lp].astype(wide)
+        first_out[:, lp * cols_f : (lp + 1) * cols_f] = f_g[lp]
+        second_out[lp * rows_s : (lp + 1) * rows_s, :] = s_g[lp]
 
 
 def sum_buffers(n_loop, n_chip, rows, cols):
@@ -402,9 +413,9 @@
     return pl.pallas_call(
         functools.partial(power_kernel, n_loop, n_chip),
         out_shape=(
-            jax.ShapeDtypeStruct((2, items, half), bf16),
-            jax.ShapeDtypeStruct((first_rows, units), jnp.float32),
-            jax.ShapeDtypeStruct((second_rows, features), jnp.float32),
+            jax.ShapeDtypeStruct((items, 2 * half), bf16),
+            jax.ShapeDtypeStruct((first_rows, units), bf16),
+            jax.ShapeDtypeStruct((second_rows, features), bf16),
         ),
         in_specs=[vmem] * 6 + [pl.BlockSpec(memory_space=pl.ANY)],
         out_specs=(vmem, vmem, vmem),
@@ -472,7 +483,7 @@
     dense = dense_pair(
         jnp.stack([index, other_index]), core, mine, other, n_loop, n_chip, items
     )
-    prop_halves, grad_first, grad_second = power_steps(
+    current, grad_first, grad_second = power_steps(
         teleport.reshape(items, 2, half).transpose(1, 0, 2),
         cotangent[0].T.reshape(2, half, items),
         flat_feats.T,
@@ -483,8 +494,7 @@
         n_loop,
         n_chip,
     )
-    current = prop_halves.transpose(1, 0, 2).reshape(items, features)
-    return (current[None], grad_first, grad_second)
+    return (current[None], grad_first.astype(jnp.float32), grad_second.astype(jnp.float32))
 
 
 def solution(mesh):

time: 130 us -> 127 us (0.977)
  local copies, waits for them, and re-layouts: 14.4 us -> 11.1 us
  other arithmetic: 2.11 us -> 5.11 us
  Pallas kernels: 110 us -> 107 us
    convert_element_type x0 -> x2, other arithmetic: none -> 3.01 us  [the longest x1 1.5 us: body(): grad_first.astype(jnp.float32)]
    unnamed x15 -> x13, local copies, waits for them, and re-layouts: 9.16 us -> 6.83 us
    pallas_call x1, Pallas kernels: 11.6 us -> 10.3 us  [dense_pair(): pl.pallas_call(dense_kernel, out_shape=jax.ShapeDtypeStruct((n_loop, n_ch...]
where the time goes in v4:
time: 127 us; the launch traced here: 126 us
  Pallas kernels  107 us (84%)
  local copies, waits for them, and re-layouts  11.1 us (9%)
  other arithmetic  5.11 us (4%)
  matrix products  1.99 us (2%)
    pallas_call x1, Pallas kernels, power_steps(): pl.pallas_call(functools.partial(power_kernel, n_loop, n_chip), out_shape...  96.7 us
    pallas_call x1, Pallas kernels, dense_pair(): pl.pallas_call(dense_kernel, out_shape=jax.ShapeDtypeStruct((n_loop, n_ch...  10.3 us
    unnamed x13, local copies, waits for them, and re-layouts  6.83 us
    ppermute x1, local copies, waits for them, and re-layouts, body(): other = lax.ppermute(mine, 'wide', swap)  2.73 us
  transfers between devices with their start and end apart: 2, of which 0 were waited for; matrix products, arithmetic and copies ran while one was open for 7% of the time, Pallas kernels for 0%

profile of v4, /device:TPU:0, one launch (start us, length us, event | category | flops | bytes accessed | tf_op | source)
XLA Modules:
  0.0 126.5 jit_solution(2970809890251578769)
XLA Ops:
  0.6 0.0 copy-start
  0.6 0.0 copy-start.3
  0.7 0.8 pad_add_fusion.1
  1.5 0.5 collective-permute-start
  2.0 0.1 collective-permute-start.1
  2.0 0.7 fusion.5
  2.8 3.7 %copy.20 = bf16[1,1,80,64,64]{4,3,2,1,0:T(8,128)(2,1)} copy(bf16[1,1,80,64,64]{2,4,3,1,0:T(8,128)(2,1)} %param.11) | data formatting | bytes 1310720 | tf_op args[4]
  6.5 0.0 copy-done.3
  6.5 0.8 copy.17
  7.2 0.0 copy-done
  7.2 0.0 copy-start.1
  7.2 1.6 %add_multiply_fusion = (f32[1024,256]{1,0:T(8,128)}, bf16[1024,256]{1,0:T(8,128)(2,1)S(1)}) fusion(bf16[256,1024]{1,0:T(8,128)(2,1)S(1)} %copy-done, bf16[1,256,256]{2,1,0:T(8,128)(2,1)S(1)} %copy-done.3), kind=kOutput, calls=%fused_computation.1 | convolution fusion | flops 136577024 | bytes 2228224 | tf_op jit(solution)/shard_map/dot_general | solution.py:475
  8.9 0.0 copy-start.2
  8.9 0.0 copy-start.4
  8.9 0.8 copy-done.2
  9.7 0.0 copy-done.1
  9.7 0.4 convolution_convert_fusion
  10.0 0.8 copy.18
  10.8 0.0 copy-done.4
  10.8 0.8 copy.19
  11.6 0.0 collective-permute-done
  11.6 0.5 pad_add_fusion.index_ref
  12.1 0.0 collective-permute-done.1
  12.1 2.7 %copy.22.other_ref = bf16[80,64,64]{2,1,0:T(8,128)(2,1)} copy(bf16[80,64,64]{0,2,1:T(8,128)(2,1)S(1)} %collective-permute-done.1) | data formatting | bytes 1310720 | tf_op jit(solution)/shard_map/ppermute | solution.py:470
  14.8 10.3 %dense_pair.1.dense_ref = bf16[4,4,2,256,512]{4,3,2,1,0:T(8,128)(2,1)} custom-call(s32[2,97]{1,0:T(2,128)} %pad_add_fusion.index_ref, s32[1]{0:T(128)} %bitcast.11.core_ref, bf16[80,64,64]{2,1,0:T(8,128)(2,1)} %bitcast.26, bf16[80,64,64]{2,1,0:T(8,128)(2,1)} %copy.22.other_ref), custom_call_target="tpu_custom_call" | custom-call | tf_op jit(solution)/shard_map/dense_pair/pallas_call | solution.py:71
  25.2 96.7 %power_steps.1 = (bf16[256,256]{1,0:T(8,128)(2,1)}, bf16[32,1024]{1,0:T(8,128)(2,1)}, bf16[128,256]{1,0:T(8,128)(2,1)}) custom-call(bf16[2,256,128]{2,1,0:T(8,128)(2,1)} %bitcast.29, bf16[2,128,256]{2,1,0:T(8,128)(2,1)} %bitcast.30, bf16[256,256]{1,0:T(8,128)(2,1)} %bitcast.28, bf16[1024,256]{1,0:T(8,128)(2,1)} %copy-done.2, ...), custom_call_target="tpu_custom_call" | custom-call | tf_op jit(solution)/shard_map/power_steps/pallas_call | solution.py:413
  121.9 1.5 %convert_element_type.14 = f32[32,1024]{1,0:T(8,128)} convert(bf16[32,1024]{1,0:T(8,128)(2,1)} %get-tuple-element.7) | non-fusion elementwise | flops 32768 | bytes 196608 | tf_op jit(solution)/shard_map/convert_element_type | solution.py:497
  123.4 1.5 %convert_element_type.15 = f32[128,256]{1,0:T(8,128)} convert(bf16[128,256]{1,0:T(8,128)(2,1)} %get-tuple-element.8) | non-fusion elementwise | flops 32768 | bytes 196608 | tf_op jit(solution)/shard_map/convert_element_type | solution.py:497
  124.9 1.6 %copy.25 = bf16[1,256,256]{2,1,0:T(8,128)(2,1)} copy(bf16[1,256,256]{2,1,0:T(8,128)(2,1)} %bitcast.33) | data formatting | bytes 262144
Async XLA Ops:
  0.6 6.6 %copy-start = (bf16[256,1024]{1,0:T(8,128)(2,1)S(1)}, bf16[256,1024]{1,0:T(8,128)(2,1)}, u32[]{:S(2)}) copy-start(bf16[256,1024]{1,0:T(8,128)(2,1)} %param.8) | copy-start | bytes 1572868
  0.6 5.8 %copy-start.3 = (bf16[1,256,256]{2,1,0:T(8,128)(2,1)S(1)}, bf16[1,256,256]{2,1,0:T(8,128)(2,1)}, u32[]{:S(2)}) copy-start(bf16[1,256,256]{2,1,0:T(8,128)(2,1)} %param.7) | copy-start | bytes 393220
  1.5 10.1 %collective-permute-start = (s32[97]{0:T(128)S(1)}, s32[97]{0:T(128)S(1)}, u32[]{:S(2)}, u32[]{:S(2)}) collective-permute-start(s32[97]{0:T(128)S(1)} %pad_add_fusion.1), channel_id=1, source_target_pairs={{0,1},{1,0},{2,3},{3,2},{4,5},{5,4},{6,7},{7,6},{8,9},{9,8},{10,11... | collective-permute-start | bytes 1172 | tf_op jit(solution)/shard_map/ppermute | solution.py:471
  2.0 10.1 %collective-permute-start.1 = (bf16[80,64,64]{0,2,1:T(8,128)(2,1)}, bf16[80,64,64]{0,2,1:T(8,128)(2,1)S(1)}, u32[]{:S(2)}, u32[]{:S(2)}) collective-permute-start(bf16[80,64,64]{0,2,1:T(8,128)(2,1)} %bitcast.27), channel_id=1, source_target_pairs={{0,1},{1,0},{2,3},{3,2},{4,5},{5,4},{6,7},{7,6},{8,9},{9,8},{10,11... | collective-permute-start | bytes 1966088 | tf_op jit(solution)/shard_map/ppermute | solution.py:470
  7.2 2.4 %copy-start.1 = (bf16[1024,256]{1,0:T(8,128)(2,1)S(1)}, bf16[1024,256]{1,0:T(8,128)(2,1)}, u32[]{:S(2)}) copy-start(bf16[1024,256]{1,0:T(8,128)(2,1)} %second_ref.1) | copy-start | bytes 1572868
  8.9 0.8 copy-start.2
  8.9 1.9 %copy-start.4 = (bf16[1,256,256]{2,1,0:T(8,128)(2,1)S(1)}, bf16[1,256,256]{2,1,0:T(8,128)(2,1)}, u32[]{:S(2)}) copy-start(bf16[1,256,256]{2,1,0:T(8,128)(2,1)} %param.10) | copy-start | bytes 393220
